TPU v7x, 32 devices: a whole 2x2x4 slice. The times are simulated.
32 devices in a mesh: seq: 4 (over y, x), fsdp: 8 (over z, core).
Axes of the slice: x: 2, y: 2, z: 4, core: 2. Of those that a mesh axis runs over, the one named last changes fastest.
Arguments:
- frames: bfloat16 [8, 2048, 1536], P('fsdp', 'seq'), may hold values from -6 to 6
- lengths: int32 [8], P('fsdp'), may hold values from 512 to 2048, as said below
- gain: float32 [1536], replicated, may hold values from 0.5 to 1.5
- w_pointwise: bfloat16 [1536, 3072], P('fsdp'), may hold values from -0.15625 to 0.15625
- w_depthwise: float32 [31, 1536], replicated, may hold values from -1 to 1
- w_output: bfloat16 [1536, 1536], P('fsdp'), may hold values from -0.15625 to 0.15625
- cotangent: bfloat16 [8, 2048, 1536], P('fsdp', 'seq'), may hold values from -6 to 6
Outputs:
- output: bfloat16 [8, 2048, 1536], P('fsdp', 'seq')
- grad_frames: bfloat16 [8, 2048, 1536], P('fsdp', 'seq')
- grad_pointwise: float32 [1536, 3072], P('fsdp')
- grad_output: float32 [1536, 1536], P('fsdp')
- grad_gain: float32 [1536], replicated
- grad_depthwise: float32 [31, 1536], replicated
Inputs may be any that keep to these rules, and one draw needn't show every extreme that they name: `lengths`: the first utterance fills all 2048 slots.
All inputs are finite; a program needn't handle non-finite values.
Results may differ from a plain program's by a relative error of at most 0.014.
Values may be sent and summed in bfloat16 or wider, within the bound.
No kernel may reach another device: no remote copies, remote signals or barrier semaphores. Data moves between devices by JAX's collectives and lax.ppermute only.
A program may use at most 128 MiB of HBM per device.

v0:
```python
import jax
import jax.numpy as jnp
from jax import lax
from jax.sharding import PartitionSpec as P

EPS = 1e-05


def extended(block, sides, width):
    for axis, dim in sides:
        count = lax.axis_size(axis)
        forward = [(i, i + 1) for i in range(count - 1)]
        backward = [(target, source) for source, target in forward]
        low = lax.ppermute(
            lax.slice_in_dim(block, block.shape[dim] - width, None, axis=dim), axis, forward
        )
        high = lax.ppermute(lax.slice_in_dim(block, 0, width, axis=dim), axis, backward)
        block = jnp.concatenate([low, block, high], axis=dim)
    return block


def rounded_term(left, right):
    term = lax.dot_general(
        left, right, (((0,), (0,)), ((), ())), preferred_element_type=jnp.float32
    )
    term = lax.optimization_barrier(term.astype(jnp.bfloat16))
    return term.astype(jnp.float32)


def on_device(frames, lengths, gain, w_pointwise, w_depthwise, w_output, cotangent):
    frame_count = frames.shape[1]
    width = frames.shape[2]
    taps = w_depthwise.shape[0]
    half_width = (taps - 1) // 2
    full_pointwise, full_output = (
        lax.all_gather(w_pointwise, "fsdp", axis=0, tiled=True),
        lax.all_gather(w_output, "fsdp", axis=0, tiled=True),
    )
    as_float = frames[0].astype(jnp.float32)
    center = jnp.mean(as_float, axis=-1, keepdims=True)
    spread = jnp.mean((as_float - center) ** 2, axis=-1, keepdims=True)
    inverse = lax.rsqrt(spread + EPS)
    normed = (as_float - center) * inverse
    lifted = (normed * gain).astype(jnp.bfloat16)
    position = lax.axis_index("seq") * frame_count + jnp.arange(frame_count, dtype=jnp.int32)
    mask = (position < lengths[0]).astype(jnp.float32)[:, None]
    joined = jnp.dot(lifted, full_pointwise, preferred_element_type=jnp.float32)
    value = joined[:, :width]
    gate_sig = jax.nn.sigmoid(joined[:, width:])
    glu = (value * gate_sig * mask).astype(jnp.bfloat16)
    glu_ext = extended(glu[None], (("seq", 1),), half_width)[0].astype(jnp.float32)
    conv = jnp.zeros((frame_count, width), jnp.float32)
    for offset in range(taps):
        conv = conv + w_depthwise[offset] * glu_ext[offset : offset + frame_count]
    conv_sig = jax.nn.sigmoid(conv)
    swished = (conv * conv_sig).astype(jnp.bfloat16)
    branch = jnp.dot(swished, full_output, preferred_element_type=jnp.float32)
    output = (as_float + branch).astype(jnp.bfloat16)
    branch_grad = (cotangent[0].astype(jnp.float32) * mask).astype(jnp.bfloat16)
    swish_grad = lax.dot_general(
        branch_grad, full_output, (((1,), (1,)), ((), ())), preferred_element_type=jnp.float32
    )
    conv_grad = (swish_grad * conv_sig * (1.0 + conv * (1.0 - conv_sig))).astype(jnp.bfloat16)
    grad_ext = extended(conv_grad[None], (("seq", 1),), half_width)[0].astype(jnp.float32)
    conv_grad_f = conv_grad.astype(jnp.float32)
    glu_grad = jnp.zeros((frame_count, width), jnp.float32)
    tap_rows = []
    for offset in range(taps):
        back = taps - 1 - offset
        glu_grad = glu_grad + w_depthwise[offset] * grad_ext[back : back + frame_count]
        tap_rows.append(jnp.sum(conv_grad_f * glu_ext[offset : offset + frame_count], axis=0))
    glu_grad = glu_grad * mask
    joined_grad = jnp.concatenate(
        [glu_grad * gate_sig, glu_grad * value * gate_sig * (1.0 - gate_sig)], axis=-1
    ).astype(jnp.bfloat16)
    lifted_grad = lax.dot_general(
        joined_grad, full_pointwise, (((1,), (1,)), ((), ())), preferred_element_type=jnp.float32
    )
    gain_term = jnp.sum(lifted_grad * normed, axis=0)
    grad_gain, grad_depthwise = lax.psum((gain_term, jnp.stack(tap_rows, axis=0)), ("seq", "fsdp"))
    scaled = lifted_grad * gain
    norm_grad = inverse * (
        scaled
        - jnp.mean(scaled, axis=-1, keepdims=True)
        - normed * jnp.mean(scaled * normed, axis=-1, keepdims=True)
    )
    grad_frames = (cotangent[0].astype(jnp.float32) + norm_grad).astype(jnp.bfloat16)
    term_pointwise = rounded_term(lifted, joined_grad)
    term_output = rounded_term(swished, branch_grad)
    owned = (
        lax.psum_scatter(
            term_pointwise.astype(jnp.bfloat16), "fsdp", scatter_dimension=0, tiled=True
        ).astype(jnp.float32),
        lax.psum_scatter(
            term_output.astype(jnp.bfloat16), "fsdp", scatter_dimension=0, tiled=True
        ).astype(jnp.float32),
    )
    grad_pointwise, grad_output = (
        lax.psum(owned[0].astype(jnp.bfloat16), "seq").astype(jnp.float32),
        lax.psum(owned[1].astype(jnp.bfloat16), "seq").astype(jnp.float32),
    )
    return (output[None], grad_frames[None], grad_pointwise, grad_output, grad_gain, grad_depthwise)


def solution(mesh):
    in_specs = (
        P("fsdp", "seq", None),
        P("fsdp"),
        P(),
        P("fsdp", None),
        P(),
        P("fsdp", None),
        P("fsdp", "seq", None),
    )
    out_specs = (
        P("fsdp", "seq", None),
        P("fsdp", "seq", None),
        P("fsdp", None),
        P("fsdp", None),
        P(),
        P(),
    )
    return jax.shard_map(
        on_device, mesh=mesh, in_specs=in_specs, out_specs=out_specs, check_vma=False
    )
```

profile of v0, /device:TPU:0, one launch (start us, length us, event | category | flops | bytes accessed | tf_op | source)
XLA Modules:
  0.0 514.9 jit_solution(6867970955985143212)
XLA Ops:
  7.2 0.0 all-gather.3.cloned.1.call-start
  7.2 0.7 all-gather.3.cloned.1.call-update
  7.9 0.0 all-gather.5.cloned.1.call-start
  8.0 0.7 all-gather.5.cloned.1.call-update
  8.7 0.0 reduce-scatter.5.cloned.1.call-start
  9.4 1.7 convert_reduce_fusion
  11.1 0.6 fusion.14
  11.7 0.3 slice_reduce_fusion.30
  12.0 91.1 %all-gather.3.cloned.1.call-done = bf16[1536,3072]{1,0:T(8,128)(2,1)} async-done(((bf16[192,3072]{1,0:T(8,128)(2,1)}), bf16[1536,3072]{1,0:T(8,128)(2,1)}) %all-gather.3.cloned.1.call-update) | async-done | bytes 9437200 | tf_op jit(solution)/shard_map/all_gather | solution.py:36
  103.1 7.7 %fusion.125 = f32[512,3072]{1,0:T(8,128)S(1)} fusion(bf16[1536,3072]{1,0:T(8,128)(2,1)} %all-gather.3.cloned.1.call-done, bf16[1,512,1536]{2,1,0:T(8,128)(2,1)S(1)} %copy-done.1, f32[1536]{0:T(1024)S(1)} %copy-done.41, f32[512]{0:T(512)S(1)} %add_rsqrt_fusion, f32[512]{0:T(512)S(1)} %broadcast_multiply_fusion.2), kind=kOutput, calls=%fused_computation.269 | convolution fusion | flops 4835770368 | bytes 17311744 | tf_op jit(solution)/shard_map/dot_general | solution.py:47
  110.9 0.8 fusion.117
  111.7 1.8 copy-done
  113.6 3.4 collective-permute-start
  117.0 1.3 collective-permute-start.1
  118.3 0.2 slice_reduce_fusion.29
  118.5 0.2 collective-permute-done
  118.7 4.3 collective-permute-done.1
  123.0 0.5 maximum_convert_fusion
  123.4 12.0 %multiply_add_fusion = f32[512,1536]{1,0:T(8,128)S(1)} fusion(f32[1,542,1536]{2,1,0:T(8,128)S(1)} %maximum_convert_fusion, f32[1536]{0:T(1024)S(1)} %get-tuple-element.69, f32[1536]{0:T(1024)S(1)} %get-tuple-element.70, f32[1536]{0:T(1024)S(1)} %get-tuple-element.41, f32[1536]{0:T(1024)S(1)} %get-tuple-element.42, f32[1536]{0:T(1024)S(1)} %get-tuple-element.43, ...), kind=kLoop, calls=%fused_computation.219 | loop fusion | flops 47972352 | bytes 100853760 | tf_op jit(solution)/shard_map/add | solution.py:54
  135.5 1.7 copy-done.4
  137.3 4.8 convolution_convert_fusion.1
  142.1 0.0 reduce-scatter.3.cloned.1.call-start
  142.1 12.8 %all-gather.5.cloned.1.call-done = bf16[1536,1536]{1,0:T(8,128)(2,1)} async-done(((bf16[192,1536]{1,0:T(8,128)(2,1)}), bf16[1536,1536]{1,0:T(8,128)(2,1)}) %all-gather.5.cloned.1.call-update) | async-done | bytes 4718608 | tf_op jit(solution)/shard_map/all_gather | solution.py:37
  155.0 12.6 %fusion.46 = (f32[1536]{0:T(1024)}, f32[1536]{0:T(1024)}, f32[1536]{0:T(1024)}, f32[1536]{0:T(1024)}, f32[1536]{0:T(1024)}, /*index=5*/f32[1536]{0:T(1024)}, f32...) fusion(f32[1,542,1536]{2,1,0:T(8,128)S(1)} %maximum_convert_fus, ...), kind=kOutput, calls=%fused_computation.84 | convolution fusion | flops 2446569984 | bytes 51986432 | tf_op jit(solution)/shard_map/dot_general | solution.py:60
  167.6 0.9 fusion.128
  168.5 3.4 collective-permute-start.2
  171.9 1.5 collective-permute-start.3
  173.4 0.3 collective-permute-done.2
  173.6 4.3 collective-permute-done.3
  177.9 2.0 maximum_convert_fusion.1
  180.0 14.3 %multiply_convert_fusion.1 = (bf16[512,1536]{1,0:T(8,128)(2,1)S(1)}, f32[512,1536]{1,0:T(8,128)S(1)}) fusion(f32[512,3072]{1,0:T(8,128)} %copy-done, f32[512]{0:T(512)S(1)} %copy-done.25, f32[1,542,1536]{2,1,0:T(8,128)S(1)} %maximum_convert_fusion.1, f32[1536]{0:T(1024)S(1)} %copy-done.20, f32[1536]{0:T(1024)S(1)} %copy-done.22, ...), kind=kLoop, calls=%fused_computation.216 | loop fusion | flops 52690944 | bytes 105574400 | tf_op jit(solution)/shard_map/convert.1
  194.4 1.3 multiply_convert_fusion
  195.8 1.1 copy-done.7
  196.9 8.1 %convolution_convert_fusion = bf16[1536,3072]{1,0:T(8,128)(2,1)} fusion(bf16[512,1536]{1,0:T(8,128)(2,1)S(1)} %multiply_convert_fusion, bf16[512,1536]{1,0:T(8,128)(2,1)S(1)} %get-tuple-element.73, bf16[1,512,1536]{2,1,0:T(8,128)(2,1)S(1)} %copy-done.2, f32[1536]{0:T(1024)S(1)} %copy-done.42, f32[512]{0:T(512)S(1)} %copy-done.44, f32[512]{0:T(512)S(1)} %copy-done.27), kind=kOutput, calls=%fused_computation.31 | convolution fusion | flops 4846780416 | bytes 14166016 | tf_op jit(solution)/shard_map/dot_general | solution.py:23
  205.0 0.0 all-reduce.6.cloned.1.call-start
  205.0 6.1 %reduce-scatter.5.cloned.1.call-done = bf16[192,1536]{1,0:T(8,128)(2,1)} async-done(((bf16[1536,1536]{1,0:T(8,128)(2,1)}), bf16[192,1536]{1,0:T(8,128)(2,1)}) %reduce-scatter.5.cloned.1.call-update) | async-done | bytes 589840 | tf_op jit(solution)/shard_map/reduce_scatter | solution.py:94
  211.1 100.1 %reduce-scatter.3.cloned.1.call-done = bf16[192,3072]{1,0:T(8,128)(2,1)} async-done(((bf16[1536,3072]{1,0:T(8,128)(2,1)}), bf16[192,3072]{1,0:T(8,128)(2,1)}) %reduce-scatter.3.cloned.1.call-update) | async-done | bytes 1179664 | tf_op jit(solution)/shard_map/reduce_scatter | solution.py:91
  311.3 0.3 all-reduce.4.cloned.1.call-start
  311.6 8.3 %fusion.47 = (f32[1536]{0:T(1024)S(1)}, f32[1536]{0:T(1024)S(1)}, f32[1536]{0:T(1024)S(1)}, f32[1536]{0:T(1024)S(1)}, f32[1536]{0:T(1024)S(1)}, /*index=5*/f32[1...) fusion(bf16[512,1536]{1,0:T(8,128)(2,1)} %get-tuple-element.80,, ...), kind=kLoop, calls=%fused_computation.85 | loop fusion | flops 29070336 | bytes 58306560 | tf_op jit(solution)/shard_map/reduce_sum | solution.py:71
  320.5 2.8 stack.127
  323.3 7.8 %fusion.115 = bf16[1,512,1536]{2,1,0:T(8,128)(2,1)} fusion(bf16[1536,1536]{1,0:T(8,128)(2,1)} %all-gather.5.cloned.1.call-done, bf16[1,512,1536]{2,1,0:T(8,128)(2,1)} %param.7, f32[512,1536]{1,0:T(8,128)} %copy-done.4), kind=kOutput, calls=%fused_computation.224 | convolution fusion | flops 2422210560 | bytes 11010048 | tf_op jit(solution)/shard_map/dot_general | solution.py:57
  331.1 8.5 %fusion.13 = (f32[1536]{0:T(1024)S(1)}, f32[512]{0:T(512)S(1)}, f32[512]{0:T(512)S(1)}, f32[512,1536]{1,0:T(8,128)S(1)}) fusion(bf16[1,512,1536]{2,1,0:T(8,128)(2,1)S(1)} %copy-done.3, f32[512]{0:T(512)S(1)} %copy-done.44, f32[512]{0:T(512)S(1)} %copy-done.27, f32[1536]{0:T(1024)S(1)} %copy-done.42, bf16[1536,3072]{1,0:T(8,128)(2,1)} %all-gather.3.cloned.1.call-done, ...), kind=kOutput, calls=%fused_computation.51 | convolution fusion | flops 4845204992 | bytes 17321984 | tf_op jit(solution)/shard_map/dot_general | solution.py:76
  339.6 2.4 fusion.118
  342.1 38.0 %psum.30 = f32[1536]{0:T(1024)} all-reduce(f32[1536]{0:T(1024)S(1)} %get-tuple-element.37), channel_id=1, replica_groups=mesh['seq'=4,'fsdp'=8] {'seq','fsdp'}, use_global_device_ids=true, to_apply=%region_9.0 | all-reduce | flops 1536 | bytes 12288 | tf_op jit(solution)/shard_map/psum | solution.py:80
  380.1 3.0 convert_element_type.88
  383.1 1.1 convert_element_type.90
  384.3 122.2 %all-reduce.4.cloned.1.call-done = f32[31,1536]{1,0:T(8,128)} async-done(((f32[31,1536]{1,0:T(8,128)}), f32[31,1536]{1,0:T(8,128)}) %all-reduce.4.cloned.1.call-update) | async-done | bytes 190480 | tf_op jit(solution)/shard_map/psum | solution.py:80
  506.5 1.6 copy.17
  (133 shorter events, 0.5 us)
Async XLA Ops:
  7.2 3.9 copy-start.1
  7.2 4.5 copy-start.12
  7.2 96.0 %copy-start.41 = (f32[1536]{0:T(1024)S(1)}, f32[1536]{0:T(1024)}, u32[]{:S(2)}) copy-start(f32[1536]{0:T(1024)} %param.9) | copy-start | bytes 18436
  7.2 95.9 %all-gather.3.cloned.1.call-start = ((), (), s32[]{:S(2)}) async-start(), calls=%async_computation.2 | async-start | bytes 10616832 | tf_op jit(solution)/shard_map/all_gather | solution.py:36
  7.9 147.0 %all-gather.5.cloned.1.call-start = ((), (), s32[]{:S(2)}) async-start(), calls=%async_computation.3 | async-start | bytes 5308416 | tf_op jit(solution)/shard_map/all_gather | solution.py:37
  8.7 202.4 %reduce-scatter.5.cloned.1.call-start = ((), (), s32[]{:S(2)}) async-start(), calls=%async_computation.5 | async-start | bytes 5308416 | tf_op jit(solution)/shard_map/reduce_scatter | solution.py:94
  11.1 99.7 %copy-start.26 = (f32[512]{0:T(512)}, f32[512]{0:T(512)S(1)}, u32[]{:S(2)}) copy-start(f32[512]{0:T(512)S(1)} %broadcast_multiply_fusion.2) | copy-start | bytes 6148
  11.7 99.2 %copy-start.43 = (f32[512]{0:T(512)}, f32[512]{0:T(512)S(1)}, u32[]{:S(2)}) copy-start(f32[512]{0:T(512)S(1)} %add_rsqrt_fusion) | copy-start | bytes 6148
  12.0 98.8 %copy-start.23 = (f32[512]{0:T(512)}, f32[512]{0:T(512)S(1)}, u32[]{:S(2)}) copy-start(f32[512]{0:T(512)S(1)} %fusion.121) | copy-start | bytes 6148
  113.6 5.2 %collective-permute-start = (bf16[1,15,1536]{2,1,0:T(8,128)(2,1)S(1)}, bf16[1,15,1536]{2,1,0:T(8,128)(2,1)S(1)}, u32[]{:S(2)}, u32[]{:S(2)}) collective-permute-start(bf16[1,15,1536]{2,1,0:T(8,128)(2,1)S(1)} %get-tuple-element.77), channel_id=1, source_target_pairs={{0,8},{8,16},{16,24},{1,9},{9,17},{17,25},{2,10},{10,18},{18,26},{... | collective-permute-start | bytes 138248 | tf_op jit(solution)/shard_map/ppermute | solution.py:14
  117.0 6.0 %collective-permute-start.1 = (bf16[1,15,1536]{2,1,0:T(8,128)(2,1)S(1)}, bf16[1,15,1536]{2,1,0:T(8,128)(2,1)S(1)}, u32[]{:S(2)}, u32[]{:S(2)}) collective-permute-start(bf16[1,15,1536]{2,1,0:T(8,128)(2,1)S(1)} %get-tuple-element.78), channel_id=1, source_target_pairs={{8,0},{16,8},{24,16},{9,1},{17,9},{25,17},{10,2},{18,10},{26,18},{... | collective-permute-start | bytes 138248 | tf_op jit(solution)/shard_map/ppermute | solution.py:17
  118.5 17.0 %copy-start.13 = (f32[1536]{0:T(1024)}, f32[1536]{0:T(1024)S(1)}, u32[]{:S(2)}) copy-start(f32[1536]{0:T(1024)S(1)} %get-tuple-element.66) | copy-start | bytes 18436
  118.5 17.0 %copy-start.15 = (f32[1536]{0:T(1024)}, f32[1536]{0:T(1024)S(1)}, u32[]{:S(2)}) copy-start(f32[1536]{0:T(1024)S(1)} %get-tuple-element.67) | copy-start | bytes 18436
  118.5 17.0 %copy-start.17 = (f32[1536]{0:T(1024)}, f32[1536]{0:T(1024)S(1)}, u32[]{:S(2)}) copy-start(f32[1536]{0:T(1024)S(1)} %get-tuple-element.68) | copy-start | bytes 18436
  118.5 17.0 %copy-start.19 = (f32[1536]{0:T(1024)}, f32[1536]{0:T(1024)S(1)}, u32[]{:S(2)}) copy-start(f32[1536]{0:T(1024)S(1)} %get-tuple-element.69) | copy-start | bytes 18436
  118.5 17.0 %copy-start.21 = (f32[1536]{0:T(1024)}, f32[1536]{0:T(1024)S(1)}, u32[]{:S(2)}) copy-start(f32[1536]{0:T(1024)S(1)} %get-tuple-element.70) | copy-start | bytes 18436
  123.4 13.8 %copy-start.5 = (bf16[1,512,1536]{2,1,0:T(8,128)(2,1)S(1)}, bf16[1,512,1536]{2,1,0:T(8,128)(2,1)}, u32[]{:S(2)}) copy-start(bf16[1,512,1536]{2,1,0:T(8,128)(2,1)} %param.13) | copy-start | bytes 4718596
  123.4 13.8 %copy-start.24 = (f32[512]{0:T(512)S(1)}, f32[512]{0:T(512)}, u32[]{:S(2)}) copy-start(f32[512]{0:T(512)} %copy-done.23) | copy-start | bytes 6148
  142.1 169.1 %reduce-scatter.3.cloned.1.call-start = ((), (), s32[]{:S(2)}) async-start(), calls=%async_computation.4 | async-start | bytes 10616832 | tf_op jit(solution)/shard_map/reduce_scatter | solution.py:91
  167.6 12.3 %copy-start.14 = (f32[1536]{0:T(1024)S(1)}, f32[1536]{0:T(1024)}, u32[]{:S(2)}) copy-start(f32[1536]{0:T(1024)} %copy-done.13) | copy-start | bytes 18436
  167.6 12.4 %copy-start.16 = (f32[1536]{0:T(1024)S(1)}, f32[1536]{0:T(1024)}, u32[]{:S(2)}) copy-start(f32[1536]{0:T(1024)} %copy-done.15) | copy-start | bytes 18436
  167.6 12.4 %copy-start.18 = (f32[1536]{0:T(1024)S(1)}, f32[1536]{0:T(1024)}, u32[]{:S(2)}) copy-start(f32[1536]{0:T(1024)} %copy-done.17) | copy-start | bytes 18436
  167.6 12.4 %copy-start.20 = (f32[1536]{0:T(1024)S(1)}, f32[1536]{0:T(1024)}, u32[]{:S(2)}) copy-start(f32[1536]{0:T(1024)} %copy-done.19) | copy-start | bytes 18436
  167.6 12.4 %copy-start.22 = (f32[1536]{0:T(1024)S(1)}, f32[1536]{0:T(1024)}, u32[]{:S(2)}) copy-start(f32[1536]{0:T(1024)} %copy-done.21) | copy-start | bytes 18436
  167.6 12.4 %copy-start.25 = (f32[512]{0:T(512)S(1)}, f32[512]{0:T(512)}, u32[]{:S(2)}) copy-start(f32[512]{0:T(512)} %copy-done.23) | copy-start | bytes 6148
  168.5 5.1 collective-permute-start.2
  171.9 6.0 %collective-permute-start.3 = (bf16[1,15,1536]{2,1,0:T(8,128)(2,1)S(1)}, bf16[1,15,1536]{2,1,0:T(8,128)(2,1)S(1)}, u32[]{:S(2)}, u32[]{:S(2)}) collective-permute-start(bf16[1,15,1536]{2,1,0:T(8,128)(2,1)S(1)} %get-tuple-element.76), channel_id=1, source_target_pairs={{8,0},{16,8},{24,16},{9,1},{17,9},{25,17},{10,2},{18,10},{26,18},{... | collective-permute-start | bytes 138248 | tf_op jit(solution)/shard_map/ppermute | solution.py:17
  177.9 16.5 %slice-start = ((s8[6291456]{0:T(1024)(128)(4,1)}), s8[4194304]{0:T(1024)(128)(4,1)S(1)}, s32[]{:S(2)}) async-start(s8[6291456]{0:T(1024)(128)(4,1)} %bitcast.526), calls=%async_computation.8 | async-start | bytes 8388608
  180.0 14.4 %slice-start.1 = ((s8[6291456]{0:T(1024)(128)(4,1)}), s8[2097152]{0:T(1024)(128)(4,1)S(1)}, s32[]{:S(2)}) async-start(s8[6291456]{0:T(1024)(128)(4,1)} %bitcast.526), calls=%async_computation.9 | async-start | bytes 4194304
  205.0 175.1 %all-reduce.6.cloned.1.call-start = ((), (), s32[]{:S(2)}) async-start(), calls=%async_computation.7 | async-start | bytes 3538944 | tf_op jit(solution)/shard_map/psum | solution.py:99
  311.2 8.7 %copy-start.40 = (f32[1536]{0:T(1024)S(1)}, f32[1536]{0:T(1024)}, u32[]{:S(2)}) copy-start(f32[1536]{0:T(1024)} %get-tuple-element.24) | copy-start | bytes 18436
  311.2 8.7 %copy-start.39 = (f32[1536]{0:T(1024)S(1)}, f32[1536]{0:T(1024)}, u32[]{:S(2)}) copy-start(f32[1536]{0:T(1024)} %get-tuple-element.25) | copy-start | bytes 18436
  311.2 8.8 %copy-start.38 = (f32[1536]{0:T(1024)S(1)}, f32[1536]{0:T(1024)}, u32[]{:S(2)}) copy-start(f32[1536]{0:T(1024)} %get-tuple-element.26) | copy-start | bytes 18436
  311.2 8.8 %copy-start.37 = (f32[1536]{0:T(1024)S(1)}, f32[1536]{0:T(1024)}, u32[]{:S(2)}) copy-start(f32[1536]{0:T(1024)} %get-tuple-element.27) | copy-start | bytes 18436
  311.2 8.8 %copy-start.36 = (f32[1536]{0:T(1024)S(1)}, f32[1536]{0:T(1024)}, u32[]{:S(2)}) copy-start(f32[1536]{0:T(1024)} %get-tuple-element.28) | copy-start | bytes 18436
  311.2 8.8 %copy-start.35 = (f32[1536]{0:T(1024)S(1)}, f32[1536]{0:T(1024)}, u32[]{:S(2)}) copy-start(f32[1536]{0:T(1024)} %get-tuple-element.29) | copy-start | bytes 18436
  311.2 8.8 %copy-start.34 = (f32[1536]{0:T(1024)S(1)}, f32[1536]{0:T(1024)}, u32[]{:S(2)}) copy-start(f32[1536]{0:T(1024)} %get-tuple-element.30) | copy-start | bytes 18436
  311.2 8.8 %copy-start.33 = (f32[1536]{0:T(1024)S(1)}, f32[1536]{0:T(1024)}, u32[]{:S(2)}) copy-start(f32[1536]{0:T(1024)} %get-tuple-element.31) | copy-start | bytes 18436
  311.3 8.8 %copy-start.32 = (f32[1536]{0:T(1024)S(1)}, f32[1536]{0:T(1024)}, u32[]{:S(2)}) copy-start(f32[1536]{0:T(1024)} %get-tuple-element.32) | copy-start | bytes 18436
  311.3 8.9 %copy-start.31 = (f32[1536]{0:T(1024)S(1)}, f32[1536]{0:T(1024)}, u32[]{:S(2)}) copy-start(f32[1536]{0:T(1024)} %get-tuple-element.33) | copy-start | bytes 18436
  311.3 8.9 %copy-start.30 = (f32[1536]{0:T(1024)S(1)}, f32[1536]{0:T(1024)}, u32[]{:S(2)}) copy-start(f32[1536]{0:T(1024)} %get-tuple-element.34) | copy-start | bytes 18436
  311.3 8.9 %copy-start.29 = (f32[1536]{0:T(1024)S(1)}, f32[1536]{0:T(1024)}, u32[]{:S(2)}) copy-start(f32[1536]{0:T(1024)} %get-tuple-element.35) | copy-start | bytes 18436
  311.3 8.9 %copy-start.28 = (f32[1536]{0:T(1024)S(1)}, f32[1536]{0:T(1024)}, u32[]{:S(2)}) copy-start(f32[1536]{0:T(1024)} %get-tuple-element.36) | copy-start | bytes 18436
  311.3 195.2 %all-reduce.4.cloned.1.call-start = ((), (), s32[]{:S(2)}) async-start(), calls=%async_computation.6 | async-start | bytes 393216 | tf_op jit(solution)/shard_map/psum | solution.py:80
  323.2 7.8 %copy-start.3 = (bf16[1,512,1536]{2,1,0:T(8,128)(2,1)S(1)}, bf16[1,512,1536]{2,1,0:T(8,128)(2,1)}, u32[]{:S(2)}) copy-start(bf16[1,512,1536]{2,1,0:T(8,128)(2,1)} %param.7) | copy-start | bytes 4718596
  323.2 7.8 %copy-start.8 = (bf16[512,1536]{1,0:T(8,128)(2,1)S(1)}, bf16[512,1536]{1,0:T(8,128)(2,1)}, u32[]{:S(2)}) copy-start(bf16[512,1536]{1,0:T(8,128)(2,1)} %copy-done.7) | copy-start | bytes 4718596
  323.3 7.8 %copy-start.10 = (bf16[512,1536]{1,0:T(8,128)(2,1)S(1)}, bf16[512,1536]{1,0:T(8,128)(2,1)}, u32[]{:S(2)}) copy-start(bf16[512,1536]{1,0:T(8,128)(2,1)} %copy-done.9) | copy-start | bytes 4718596
  331.1 8.6 %copy-start.6 = (bf16[1,512,1536]{2,1,0:T(8,128)(2,1)S(1)}, bf16[1,512,1536]{2,1,0:T(8,128)(2,1)}, u32[]{:S(2)}) copy-start(bf16[1,512,1536]{2,1,0:T(8,128)(2,1)} %param.13) | copy-start | bytes 4718596
  (9 other events, 19.9 us)
Sparse Core Ops, SparseCore 0:
  9.7 93.4 all-gather.2
  104.8 50.1 all-gather.4
  157.3 53.7 reduce-scatter.4
  213.2 97.8 reduce-scatter.2
  314.2 62.9 all-reduce.5
  383.2 123.2 all-reduce.3
where the time goes:
time: 516 us; the launch traced here: 515 us
  waiting for transfers between devices  343 us (66%)
  matrix products  49.4 us (10%)
  other arithmetic  48.1 us (9%)
  blocking collectives  38 us (7%)
  between operations  15.8 us (3%)
  local copies, waits for them, and re-layouts  10.9 us (2%)
  starting transfers between devices  10 us (2%)
    psum x1, waiting for transfers between devices, on_device(): lax.psum((gain_term, jnp.stack(tap_rows, axis=0)), ('seq', 'fsdp'))  122 us
    reduce_scatter x1, waiting for transfers between devices, on_device(): lax.psum_scatter(term_pointwise.astype(jnp.bfloat16), 'fsdp', scatter_dim...  100 us
    all_gather x1, waiting for transfers between devices, on_device(): lax.all_gather(w_pointwise, 'fsdp', axis=0, tiled=True)  91.1 us
    psum x1, blocking collectives, on_device(): lax.psum((gain_term, jnp.stack(tap_rows, axis=0)), ('seq', 'fsdp'))  38 us
    another operation x2, other arithmetic  15.6 us
    dot_general x2, matrix products, rounded_term(): lax.dot_general(left, right, (((0,), (0,)), ((), ())), preferred_element_...  12.9 us
    all_gather x1, waiting for transfers between devices, on_device(): lax.all_gather(w_output, 'fsdp', axis=0, tiled=True)  12.8 us
    dot_general x1, matrix products, on_device(): lax.dot_general(branch_grad, full_output, (((1,), (1,)), ((), ())), prefe...  12.6 us
  transfers between devices with their start and end apart: 10, of which 9 were waited for; matrix products, arithmetic and copies ran while one was open for 20% of the time, Pallas kernels for 0%

commit v1 on v0

--- a/solution.py
+++ b/solution.py
@@ -1,12 +1,423 @@
+import functools
+
 import jax
 import jax.numpy as jnp
 from jax import lax
+from jax.experimental import pallas as pl
+from jax.experimental.pallas import tpu as pltpu
 from jax.sharding import PartitionSpec as P
 
 EPS = 1e-05
-
-
-def extended(block, sides, width):
+BF = jnp.bfloat16
+F32 = jnp.float32
+BOTH = ("seq", "fsdp")
+N_SEQ, N_Z, N_CORE = 4, 4, 2
+VMEM_LIMIT = 60 * 1024 * 1024
+
+
+def device_pairs(move):
+    def flat(s, z, c):
+        return (s * N_Z + z) * N_CORE + c
+    return [
+        (flat(s, z, c), flat(*move(s, z, c)))
+        for s in range(N_SEQ) for z in range(N_Z) for c in range(N_CORE)
+    ]
+
+
+ACROSS = {
+    "core": device_pairs(lambda s, z, c: (s, z, 1 - c)),
+    "x": device_pairs(lambda s, z, c: (s ^ 1, z, c)),
+    "y": device_pairs(lambda s, z, c: (s ^ 2, z, c)),
+    "d": device_pairs(lambda s, z, c: (s ^ 3, z, c)),
+    "z1": device_pairs(lambda s, z, c: (s, (z + 1) % N_Z, c)),
+    "z2": device_pairs(lambda s, z, c: (s, (z + 2) % N_Z, c)),
+    "z3": device_pairs(lambda s, z, c: (s, (z + 3) % N_Z, c)),
+}
+
+
+def send(block, way):
+    return lax.ppermute(block, BOTH, ACROSS[way])
+
+
+def part(block, index, size, axis):
+    return lax.dynamic_slice_in_dim(block, index * size, size, axis)
+
+
+def hint(bytes_accessed=1024):
+    return pl.CostEstimate(flops=0, bytes_accessed=bytes_accessed, transcendentals=0)
+
+
+def joined_kernel(j, behind, first_call, where_ref, lifted_ref, *refs):
+    own, came = refs[0:2], refs[2:4]
+    count = 2 if j == 3 else 1
+    mine, other = refs[4:4 + count], refs[4 + count:4 + 2 * count]
+    w_value_ref, w_gate_ref, value_ref, sig_ref, glu_ref = refs[-5:]
+    z, c, valid = where_ref[1], where_ref[2], where_ref[3]
+    rows = own[0].shape[0]
+    outs = w_value_ref, w_gate_ref
+    for source, pieces, core in ((own, mine, c), (came, other, 1 - c)):
+        at = pl.multiple_of((z * N_CORE + core) * rows, 64)
+        for side in range(2):
+            outs[side][pl.ds(at, rows), :] = source[side][...]
+        for index, k in enumerate(behind):
+            at = (lax.rem(z + N_Z - k, N_Z) * N_CORE + core) * rows
+            part_rows = rows // count
+            for n in range(count):
+                low = pl.ds(pl.multiple_of(at + n * part_rows, 32), part_rows)
+                for side in range(2):
+                    outs[side][low, :] = pieces[n][index, side]
+    value = jnp.dot(lifted_ref[...], w_value_ref[...], preferred_element_type=F32)
+    value_ref[...] = value
+    sig = jax.nn.sigmoid(jnp.dot(lifted_ref[...], w_gate_ref[...], preferred_element_type=F32))
+    sig_ref[...] = sig
+    position = lax.broadcasted_iota(jnp.int32, sig.shape, 0)
+    glu_ref[...] = jnp.where(position < valid, value * sig, 0.0).astype(BF)
+
+
+def joined_call(j, behind, where, lifted, w_own, w_came, mine, other, buffers):
+    frames, width = lifted.shape
+    block = width // N_SEQ
+    rows = w_own.shape[0]
+    whole = lambda a: pl.BlockSpec(a.shape, lambda i, at: (0,) * a.ndim)
+    column = lambda n: pl.BlockSpec((n, block), lambda i, at: (0, at[0] ^ j))
+    second = pl.BlockSpec((rows, block), lambda i, at: (0, N_SEQ + (at[0] ^ j)))
+    operands = [lifted, w_own, w_own, w_came, w_came, *mine, *other]
+    specs = [whole(lifted), column(rows), second, column(rows), second]
+    specs += [whole(a) for a in (*mine, *other)]
+    aliases = {}
+    if buffers:
+        aliases = {1 + len(operands) + n: n for n in range(5)}
+        operands += buffers
+        specs += [pl.BlockSpec(memory_space=pl.ANY)] * 5
+    return pl.pallas_call(
+        functools.partial(joined_kernel, j, behind, not buffers),
+        grid_spec=pltpu.PrefetchScalarGridSpec(
+            num_scalar_prefetch=1, grid=(1,), in_specs=specs,
+            out_specs=[column(width), column(width), column(frames), column(frames), column(frames)],
+        ),
+        out_shape=[
+            jax.ShapeDtypeStruct((width, width), BF), jax.ShapeDtypeStruct((width, width), BF),
+            jax.ShapeDtypeStruct((frames, width), F32), jax.ShapeDtypeStruct((frames, width), F32),
+            jax.ShapeDtypeStruct((frames, width), BF),
+        ],
+        input_output_aliases=aliases,
+        compiler_params=pltpu.CompilerParams(vmem_limit_bytes=VMEM_LIMIT),
+        cost_estimate=hint(),
+        name="joined_%d" % j,
+    )(where, *operands)
+
+
+EDGE = 16
+LANES = 128
+SUB = 8
+
+
+def extend(ext_ref, low, body, high):
+    count = body.shape[0]
+    ext_ref[0:EDGE, :] = low.astype(F32)
+    ext_ref[EDGE:EDGE + count, :] = body.astype(F32)
+    ext_ref[EDGE + count:, :] = high.astype(F32)
+
+
+def tap_sum(ext_ref, wide, first, height, order):
+    total = None
+    for o, k in enumerate(order):
+        rows = ext_ref[pl.ds(first + (o + 1), height), :]
+        term = rows.reshape(height // SUB, SUB, LANES) * wide[k][None]
+        total = term if total is None else total + term
+    return total.reshape(height, LANES)
+
+
+def widened(taps_ref, lanes):
+    return [jnp.broadcast_to(taps_ref[k:k + 1, lanes], (SUB, LANES)) for k in range(taps_ref.shape[0])]
+
+
+def forward_kernel(glu_ref, low_ref, high_ref, taps_ref, swished_ref, slope_ref, ext_ref):
+    frames, width = glu_ref.shape
+    height = 64
+
+    @pl.loop(0, width // LANES)
+    def _(b):
+        lanes = pl.ds(pl.multiple_of(b * LANES, LANES), LANES)
+        wide = widened(taps_ref, lanes)
+        extend(ext_ref, low_ref[:, lanes], glu_ref[:, lanes], high_ref[:, lanes])
+
+        @pl.loop(0, frames // height)
+        def _(i):
+            first = pl.multiple_of(i * height, height)
+            conv = tap_sum(ext_ref, wide, first, height, range(len(wide)))
+            sig = jax.nn.sigmoid(conv)
+            at = pl.ds(first, height)
+            swished_ref[at, lanes] = (conv * sig).astype(BF)
+            slope_ref[at, lanes] = sig * (1.0 + conv * (1.0 - sig))
+
+
+def forward_call(glu, low, high, taps):
+    frames, width = glu.shape
+    size = width // N_SEQ
+    column = lambda rows: pl.BlockSpec((rows, size), lambda i: (0, i))
+    return pl.pallas_call(
+        forward_kernel,
+        grid=(width // size,),
+        out_shape=(jax.ShapeDtypeStruct((frames, width), BF), jax.ShapeDtypeStruct((frames, width), F32)),
+        in_specs=[column(frames), column(EDGE), column(EDGE), column(taps.shape[0])],
+        out_specs=(column(frames),) * 2,
+        scratch_shapes=[pltpu.VMEM((frames + 2 * EDGE, LANES), F32)],
+        compiler_params=pltpu.CompilerParams(vmem_limit_bytes=VMEM_LIMIT),
+        cost_estimate=hint(),
+        name="conv_forward",
+    )(glu, low, high, taps)
+
+
+def backward_kernel(
+    where_ref, grad_ref, grad_low_ref, grad_high_ref, glu_ref, low_ref, high_ref, taps_ref, value_ref, sig_ref, *refs
+):
+    mine_ref, send_ref, value_grad_ref, gate_grad_ref, tap_grad_ref, ext_ref, sum_ref = refs[-7:]
+    frames, width = glu_ref.shape
+    taps = taps_ref.shape[0]
+    height = 64
+    c, valid = where_ref[2], where_ref[3]
+
+    @pl.loop(0, width // LANES)
+    def _(b):
+        lanes = pl.ds(pl.multiple_of(b * LANES, LANES), LANES)
+        wide = widened(taps_ref, lanes)
+        extend(ext_ref, grad_low_ref[:, lanes], grad_ref[:, lanes], grad_high_ref[:, lanes])
+
+        @pl.loop(0, frames // height)
+        def _(i):
+            first = pl.multiple_of(i * height, height)
+            at = pl.ds(first, height)
+            glu_grad = tap_sum(ext_ref, wide, first, height, range(taps - 1, -1, -1))
+            position = first + lax.broadcasted_iota(jnp.int32, (height, LANES), 0)
+            sig = sig_ref[at, lanes]
+            scaled = jnp.where(position < valid, glu_grad, 0.0) * sig
+            by_gate = (scaled * value_ref[at, lanes] * (1.0 - sig)).astype(BF)
+            scaled = scaled.astype(BF)
+            value_grad_ref[at, lanes] = scaled
+            gate_grad_ref[at, lanes] = by_gate
+            mine_ref[at, lanes] = jnp.where(c == 0, scaled, by_gate)
+            send_ref[at, lanes] = jnp.where(c == 0, by_gate, scaled)
+
+        extend(ext_ref, low_ref[:, lanes], glu_ref[:, lanes], high_ref[:, lanes])
+        sum_ref[...] = jnp.zeros_like(sum_ref)
+
+        @pl.loop(0, frames // height)
+        def _(i):
+            first = pl.multiple_of(i * height, height)
+            grad = grad_ref[pl.ds(first, height), lanes].astype(F32)
+            for k in range(taps):
+                term = grad * ext_ref[pl.ds(first + (k + 1), height), :]
+                sum_ref[k] += jnp.sum(term.reshape(height // SUB, SUB, LANES), axis=0)
+
+        tap_grad_ref[:, lanes] = jnp.sum(sum_ref[...], axis=1)
+
+
+def backward_call(j, where, grad, grad_low, grad_high, glu, low, high, taps, value, sig, buffers):
+    frames, width = glu.shape
+    size = width // N_SEQ
+    count = taps.shape[0]
+    column = lambda rows: pl.BlockSpec((rows, size), lambda i, at: (0, at[0] ^ j))
+    alone = pl.BlockSpec((frames, size), lambda i, at: (0, 0))
+    operands = [grad, grad_low, grad_high, glu, low, high, taps, value, sig]
+    specs = [column(n) for n in (frames, EDGE, EDGE, frames, EDGE, EDGE, count, frames, frames)]
+    aliases = {}
+    if buffers:
+        aliases = {1 + len(operands) + n: 2 + n for n in range(3)}
+        operands += buffers
+        specs += [pl.BlockSpec(memory_space=pl.ANY)] * 3
+    small = jax.ShapeDtypeStruct((frames, size), BF)
+    full = jax.ShapeDtypeStruct((frames, width), BF)
+    mine, sent, *buffers = pl.pallas_call(
+        backward_kernel,
+        grid_spec=pltpu.PrefetchScalarGridSpec(
+            num_scalar_prefetch=1, grid=(1,), in_specs=specs,
+            out_specs=[alone, alone, column(frames), column(frames), column(count + 1)],
+            scratch_shapes=[
+                pltpu.VMEM((frames + 2 * EDGE, LANES), F32), pltpu.VMEM((count + 1, SUB, LANES), F32),
+            ],
+        ),
+        out_shape=[small, small, full, full, jax.ShapeDtypeStruct((count + 1, width), F32)],
+        input_output_aliases=aliases,
+        compiler_params=pltpu.CompilerParams(vmem_limit_bytes=VMEM_LIMIT),
+        cost_estimate=hint(),
+        name="conv_backward_%d" % j,
+    )(where, *operands)
+    return mine, sent, buffers
+
+
+def edges(block):
+    count = lax.axis_size("seq")
+    forward = [(i, i + 1) for i in range(count - 1)]
+    backward = [(target, source) for source, target in forward]
+    return (
+        lax.ppermute(block[block.shape[0] - EDGE:], "seq", forward),
+        lax.ppermute(block[:EDGE], "seq", backward),
+    )
+
+
+def transposed_dot(left, right):
+    return lax.dot_general(left, right, (((0,), (0,)), ((), ())), preferred_element_type=F32)
+
+
+def final_kernel(block, where_ref, *refs):
+    pieces, (pointwise_ref, output_ref) = refs[:-2], refs[-2:]
+    s = where_ref[0]
+    width = N_SEQ * block
+    for j in range(N_SEQ):
+        for side in range(2):
+            at = pl.multiple_of(side * width + (s ^ j) * block, 128)
+            pointwise_ref[:, pl.ds(at, block)] = pieces[j][side].astype(F32)
+        rows = pieces[N_SEQ + j].shape[0]
+        output_ref[pl.ds(pl.multiple_of((s ^ j) * rows, 16), rows), :] = pieces[N_SEQ + j][...].astype(F32)
+
+
+def final_call(where, block, pointwise_pieces, output_pieces):
+    width = N_SEQ * block
+    rows = pointwise_pieces[0].shape[1]
+    vmem = pl.BlockSpec(memory_space=pltpu.VMEM)
+    operands = (*pointwise_pieces, *output_pieces)
+    return pl.pallas_call(
+        functools.partial(final_kernel, block),
+        out_shape=(
+            jax.ShapeDtypeStruct((rows, 2 * width), F32),
+            jax.ShapeDtypeStruct((rows, width), F32),
+        ),
+        in_specs=[pl.BlockSpec(memory_space=pltpu.SMEM)] + [vmem] * len(operands),
+        out_specs=(vmem, vmem),
+        compiler_params=pltpu.CompilerParams(vmem_limit_bytes=VMEM_LIMIT),
+        cost_estimate=hint(),
+        name="final",
+    )(where, *operands)
+
+
+def after(values, *first):
+    return lax.optimization_barrier((values, first))[0]
+
+
+def on_slice(frames, lengths, gain, w_pointwise, w_depthwise, w_output, cotangent):
+    frame_count, width = frames.shape[1:]
+    taps = w_depthwise.shape[0]
+    block = width // N_SEQ
+    rows = width // (N_Z * N_CORE)
+    s = lax.axis_index("seq")
+    z, c = lax.axis_index("fsdp") // N_CORE, lax.axis_index("fsdp") % N_CORE
+    where = jnp.stack([s, z, c, lengths[0] - s * frame_count]).astype(jnp.int32)
+
+    first = jnp.stack([
+        lax.dynamic_slice_in_dim(w_pointwise, s * block, block, 1),
+        lax.dynamic_slice_in_dim(w_pointwise, width + s * block, block, 1),
+    ])
+    behind = (1, 3, 2)
+    group = [send(first, "z%d" % k) for k in behind]
+    w_came = send(w_pointwise, "core")
+    as_float = frames[0].astype(F32)
+    center = jnp.mean(as_float, axis=-1, keepdims=True)
+    spread = jnp.mean((as_float - center) ** 2, axis=-1, keepdims=True)
+    inverse = lax.rsqrt(spread + EPS)
+    normed = (as_float - center) * inverse
+    lifted = (normed * gain).astype(BF)
+    position = jnp.arange(frame_count, dtype=jnp.int32)
+    mask = (position < where[3]).astype(F32)[:, None]
+    branch_grad = (cotangent[0].astype(F32) * mask).astype(BF)
+    group, lifted, branch_grad, w_came = lax.optimization_barrier(
+        (jnp.stack(group), lifted, branch_grad, w_came)
+    )
+    full_output = lax.all_gather(after(w_output, group), "fsdp", axis=0, tiled=True)
+
+    from_x, from_y = send(group, "x"), send(group, "y")
+    lifted_other = send(lifted, "core")
+    group_other = send(group, "core")
+    turned, turned_other = lifted.T, lifted_other.T
+    from_x, from_y, turned, turned_other, group_other = lax.optimization_barrier(
+        (from_x, from_y, turned, turned_other, group_other)
+    )
+    top, bottom = send(from_x[:, :, :rows // 2], "y"), send(from_y[:, :, rows // 2:], "x")
+    from_x_other, from_y_other = send(from_x, "core"), send(from_y, "core")
+    buffers = []
+    for j, mine, other in ((0, group, group_other), (1, from_x, from_x_other), (2, from_y, from_y_other)):
+        buffers = joined_call(j, behind, where, lifted, w_pointwise, w_came, [mine], [other], buffers)
+    top, bottom, buffers = lax.optimization_barrier((top, bottom, buffers))
+    top_other, bottom_other = send(top, "core"), send(bottom, "core")
+    buffers = joined_call(
+        3, behind, where, lifted, w_pointwise, w_came, [top, bottom], [top_other, bottom_other], buffers
+    )
+    w_value, w_gate, value, gate_sig, glu = buffers
+
+    glu_low, glu_high = edges(glu)
+    swished, slope = forward_call(glu, glu_low, glu_high, w_depthwise)
+    contract = (((1,), (1,)), ((), ()))
+    swish_grad = lax.dot_general(branch_grad, full_output, contract, preferred_element_type=F32)
+    conv_grad = (swish_grad * slope).astype(BF)
+    grad_low, grad_high = edges(conv_grad)
+    term_output = transposed_dot(after(swished, conv_grad), branch_grad).astype(BF)
+    grad_low, grad_high, term_output = lax.optimization_barrier((grad_low, grad_high, term_output))
+    owned_output = lax.psum_scatter(term_output, "fsdp", scatter_dimension=0, tiled=True)
+    branch = jnp.dot(swished, full_output, preferred_element_type=F32)
+    output = (as_float + branch).astype(BF)
+
+    buffers, terms, came = [], {}, {}
+    waits = {2: 3, 0: 1}
+    for j, way in ((3, "d"), (1, "x"), (2, "y"), (0, None)):
+        if j in waits:
+            buffers = after(buffers, terms[waits[j]])
+        mine, sent, buffers = backward_call(
+            j, where, conv_grad, grad_low, grad_high, glu, glu_low, glu_high, w_depthwise, value, gate_sig, buffers
+        )
+        other = send(sent, "core")
+        term = jnp.dot(turned, mine, preferred_element_type=F32) + jnp.dot(
+            turned_other, other, preferred_element_type=F32
+        )
+        terms[j] = term.astype(BF) if j else term
+        if way:
+            came[j] = send(terms[j], way)
+    grad_value, grad_gate, tap_grad = buffers
+
+    grad_value, grad_gate = after((grad_value, grad_gate), terms[2])
+    lifted_grad = lax.dot_general(
+        grad_value, w_value, contract, preferred_element_type=F32
+    ) + lax.dot_general(grad_gate, w_gate, contract, preferred_element_type=F32)
+    gain_term = jnp.sum(lifted_grad * normed, axis=0)
+    small = jnp.concatenate([tap_grad[:taps], gain_term[None]], axis=0)
+
+    total = (terms[0] + came[1].astype(F32) + came[2].astype(F32) + came[3].astype(F32)).astype(BF)
+    total, small, lifted_grad, owned_output = lax.optimization_barrier((total, small, lifted_grad, owned_output))
+    own = part(total, z, 2 * rows, 0)
+    over_z = [send(part(total, (z + k) % N_Z, 2 * rows, 0), "z%d" % k) for k in (2, 1, 3)]
+    scaled = lifted_grad * gain
+    norm_grad = inverse * (
+        scaled
+        - jnp.mean(scaled, axis=-1, keepdims=True)
+        - normed * jnp.mean(scaled * normed, axis=-1, keepdims=True)
+    )
+    grad_frames = (cotangent[0].astype(F32) + norm_grad).astype(BF)
+    quarter = rows // N_SEQ
+    own_output = part(owned_output, s, quarter, 0).astype(F32)
+    for j, way in ((3, "d"), (1, "x"), (2, "y")):
+        own_output = own_output + send(part(owned_output, s ^ j, quarter, 0), way).astype(F32)
+    own_output = own_output.astype(BF)
+    output_pieces = [own_output] + [send(own_output, way) for way in ("x", "y", "d")]
+    for way in ("core", "x", "y"):
+        small = small + send(small, way)
+    over_z, own, small, grad_frames, output_pieces = lax.optimization_barrier(
+        (over_z, own, small, grad_frames, output_pieces)
+    )
+
+    own = own.astype(F32)
+    for piece in over_z:
+        own = own + piece.astype(F32)
+    own = own.astype(BF)
+    kept, theirs = part(own, c, rows, 0), part(own, 1 - c, rows, 0)
+    swapped = send(theirs, "core")
+    pair = jnp.stack([jnp.where(c == 0, kept, swapped), jnp.where(c == 0, swapped, kept)])
+    pieces = [pair] + [send(pair, way) for way in ("x", "y", "d")]
+    turn = small + send(small, "z2")
+    small = turn + send(turn, "z1")
+    grad_pointwise, grad_output = final_call(where, block, pieces, output_pieces)
+    return (output[None], grad_frames[None], grad_pointwise, grad_output, small[taps], small[:taps])
+
+
+def extended_plain(block, sides, width):
     for axis, dim in sides:
         count = lax.axis_size(axis)
         forward = [(i, i + 1) for i in range(count - 1)]
@@ -27,7 +438,7 @@
     return term.astype(jnp.float32)
 
 
-def on_device(frames, lengths, gain, w_pointwise, w_depthwise, w_output, cotangent):
+def on_any_mesh(frames, lengths, gain, w_pointwise, w_depthwise, w_output, cotangent):
     frame_count = frames.shape[1]
     width = frames.shape[2]
     taps = w_depthwise.shape[0]
@@ -48,7 +459,7 @@
     value = joined[:, :width]
     gate_sig = jax.nn.sigmoid(joined[:, width:])
     glu = (value * gate_sig * mask).astype(jnp.bfloat16)
-    glu_ext = extended(glu[None], (("seq", 1),), half_width)[0].astype(jnp.float32)
+    glu_ext = extended_plain(glu[None], (("seq", 1),), half_width)[0].astype(jnp.float32)
     conv = jnp.zeros((frame_count, width), jnp.float32)
     for offset in range(taps):
         conv = conv + w_depthwise[offset] * glu_ext[offset : offset + frame_count]
@@ -61,7 +472,7 @@
         branch_grad, full_output, (((1,), (1,)), ((), ())), preferred_element_type=jnp.float32
     )
     conv_grad = (swish_grad * conv_sig * (1.0 + conv * (1.0 - conv_sig))).astype(jnp.bfloat16)
-    grad_ext = extended(conv_grad[None], (("seq", 1),), half_width)[0].astype(jnp.float32)
+    grad_ext = extended_plain(conv_grad[None], (("seq", 1),), half_width)[0].astype(jnp.float32)
     conv_grad_f = conv_grad.astype(jnp.float32)
     glu_grad = jnp.zeros((frame_count, width), jnp.float32)
     tap_rows = []
@@ -120,6 +531,8 @@
         P(),
         P(),
     )
+    known = mesh.shape["seq"] == N_SEQ and mesh.shape["fsdp"] == N_Z * N_CORE
     return jax.shard_map(
-        on_device, mesh=mesh, in_specs=in_specs, out_specs=out_specs, check_vma=False
-    )
+        on_slice if known else on_any_mesh,
+        mesh=mesh, in_specs=in_specs, out_specs=out_specs, check_vma=False,
+    )

time: 516 us -> 292 us (0.57)
  waiting for transfers between devices: 343 us -> 81.7 us
  Pallas kernels: 0 us -> 70.7 us
  starting transfers between devices: 10 us -> 53.5 us
  blocking collectives: 38 us -> 0 us
  other arithmetic: 48.1 us -> 16.2 us
  matrix products: 49.4 us -> 40.3 us
    psum x2 -> x0, waiting for transfers between devices: 122 us -> none  [the longest x1 122 us: on_device(): lax.psum((gain_term, jnp.stack(tap_rows, axis=0)), ('seq', 'fsdp'))]
    reduce_scatter x2 -> x1, waiting for transfers between devices: 106 us -> 0.01 us  [on_slice(): lax.psum_scatter(term_output, 'fsdp', scatter_dimension=0, tiled=True)]
    all_gather x2 -> x1, waiting for transfers between devices: 104 us -> 0.01 us  [on_slice(): lax.all_gather(after(w_output, group), 'fsdp', axis=0, tiled=True)]
    ppermute x4 -> x43, waiting for transfers between devices: 8.93 us -> 81.6 us  [the longest x39 76.8 us: send(): return lax.ppermute(block, BOTH, ACROSS[way])]
    pallas_call x0 -> x10, Pallas kernels: none -> 70.7 us  [the longest x4 32.2 us: backward_call(): pl.pallas_call(backward_kernel, grid_spec=pltpu.PrefetchScalarGridSpec(nu...]
    ppermute x4 -> x43, starting transfers between devices: 9.56 us -> 53.4 us  [the longest x39 43.8 us: send(): return lax.ppermute(block, BOTH, ACROSS[way])]
    psum x1 -> x0, blocking collectives: 38 us -> none  [on_device(): lax.psum((gain_term, jnp.stack(tap_rows, axis=0)), ('seq', 'fsdp'))]
    another operation x2 -> x5, other arithmetic: 15.6 us -> 3.45 us  [the longest x1 2 us: on_slice(): jnp.stack(group)]
  transfers between devices with their start and end apart: 10 -> 45, of which waited for: 9 -> 17; matrix products, arithmetic and copies ran while one was open for 20% -> 19% of each run, Pallas kernels for 0% -> 23%
where the time goes in v1:
time: 292 us; the launch traced here: 291 us
  waiting for transfers between devices  81.7 us (28%)
  Pallas kernels  70.7 us (24%)
  starting transfers between devices  53.5 us (18%)
  matrix products  40.3 us (14%)
  other arithmetic  16.2 us (6%)
  between operations  15.3 us (5%)
  local copies, waits for them, and re-layouts  13.2 us (5%)
    ppermute x39, waiting for transfers between devices, send(): return lax.ppermute(block, BOTH, ACROSS[way])  76.8 us
    ppermute x39, starting transfers between devices, send(): return lax.ppermute(block, BOTH, ACROSS[way])  43.8 us
    pallas_call x4, Pallas kernels, backward_call(): pl.pallas_call(backward_kernel, grid_spec=pltpu.PrefetchScalarGridSpec(nu...  32.2 us
    pallas_call x4, Pallas kernels, joined_call(): pl.pallas_call(functools.partial(joined_kernel, j, behind, not buffers),...  22.8 us
    pallas_call x1, Pallas kernels, forward_call(): pl.pallas_call(forward_kernel, grid=(width // size,), out_shape=(jax.Shap...  12.3 us
    dot_general x4, matrix products, on_slice(): jnp.dot(turned, mine, preferred_element_type=F32)  9.27 us
    ppermute x2, starting transfers between devices, edges(): lax.ppermute(block[block.shape[0] - EDGE:], 'seq', forward)  6.9 us
    dot_general x1, matrix products, on_slice(): branch = jnp.dot(swished, full_output, preferred_element_type=F32)  6.57 us
  transfers between devices with their start and end apart: 45, of which 17 were waited for; matrix products, arithmetic and copies ran while one was open for 19% of the time, Pallas kernels for 23%

profile of v1, /device:TPU:0, one launch (start us, length us, event | category | flops | bytes accessed | tf_op | source)
XLA Modules:
  0.0 290.8 jit_solution(7108624213961082657)
XLA Ops:
  9.1 4.0 %collective-permute-start.2 = (bf16[2,192,384]{2,1,0:T(8,128)(2,1)}, bf16[2,192,384]{2,1,0:T(8,128)(2,1)S(1)}, u32[]{:S(2)}, u32[]{:S(2)}) collective-permute-start(bf16[2,192,384]{2,1,0:T(8,128)(2,1)} %pad_maximum_fusion.1), channel_id=1, source_target_pairs={{0,4},{1,5},{2,6},{3,7},{4,0},{5,1},{6,2},{7,3},{8,12},{9,13},{10,... | collective-permute-start | bytes 884744 | tf_op jit(solution)/shard_map/ppermute | solution.py:39
  13.2 1.6 collective-permute-start
  14.7 2.2 collective-permute-start.1
  17.0 1.7 convert_reduce_fusion
  19.9 3.8 %fusion.8 = (bf16[512,1536]{1,0:T(8,128)(2,1)S(1)}, bf16[512,1536]{1,0:T(8,128)(2,1)}) fusion(bf16[1,512,1536]{2,1,0:T(8,128)(2,1)} %param.7, f32[1536]{0:T(1024)S(1)} %copy-done.34, f32[512]{0:T(512)S(1)} %add_rsqrt_fusion, f32[512]{0:T(512)S(1)} %broadcast_multiply_fusion.2, f32[512]{0:T(512)S(1)} %fusion.26, bf16[1,512,1536]{2,1,0:T(8,128)(2,1)} %param.13), kind=kLoop, calls=%fused_computation.15 | loop fusion | flops 6291456 | bytes 6303744 | tf_op jit(solution)/shard_map/convert_element_type | solution.py:319
  23.7 10.1 %collective-permute-done.2 = bf16[2,192,384]{2,1,0:T(8,128)(2,1)S(1)} collective-permute-done((bf16[2,192,384]{2,1,0:T(8,128)(2,1)}, bf16[2,192,384]{2,1,0:T(8,128)(2,1)S(1)}, u32[]{:S(2)}, u32[]{:S(2)}) %collective-permute-start.2) | collective-permute-done | bytes 294944 | tf_op jit(solution)/shard_map/ppermute | solution.py:39
  34.7 2.0 pad_maximum_fusion.refs_4_
  37.7 1.5 collective-permute-start.4
  39.3 1.5 collective-permute-start.5
  40.8 19.3 %collective-permute-done.4.refs_4_ = bf16[3,2,192,384]{3,2,1,0:T(8,128)(2,1)} collective-permute-done((bf16[3,2,192,384]{3,2,1,0:T(8,128)(2,1)}, bf16[3,2,192,384]{3,2,1,0:T(8,128)(2,1)}, u32[]{:S(2)}, u32[]{:S(2)}) %collective-permute-start.4) | collective-permute-done | bytes 884768 | tf_op jit(solution)/shard_map/ppermute | solution.py:39
  62.8 1.8 slice.27
  64.6 1.8 slice.28
  66.5 1.5 collective-permute-start.8
  69.1 5.7 %joined_0.1 = (bf16[1536,1536]{1,0:T(8,128)(2,1)}, bf16[1536,1536]{1,0:T(8,128)(2,1)}, f32[512,1536]{1,0:T(8,128)}, f32[512,1536]{1,0:T(8,128)}, bf16[512,1536]{1,0:T(8,128)(2,1)}) custom-call(s32[4]{0:T(128)} %pad_add_fusion.where_ref, bf16[512,1536]{1,0:T(8,128)(2,1)} %copy-done, bf16[192,3072]{1,0:T(8,128)(2,1)} %refs_1_.7, bf16[192,3072]{1,0:T(8,128)(2,1)} %refs_1_.7, ...), custom_call_target="tpu_custom_call" | custom-call | bytes 1024 | tf_op jit(solution)/shard_map/joined_0/pallas_call | solution.py:92
  74.8 5.7 %joined_1.1 = (bf16[1536,1536]{1,0:T(8,128)(2,1)}, bf16[1536,1536]{1,0:T(8,128)(2,1)}, f32[512,1536]{1,0:T(8,128)}, f32[512,1536]{1,0:T(8,128)}, bf16[512,1536]{1,0:T(8,128)(2,1)}) custom-call(s32[4]{0:T(128)} %pad_add_fusion.where_ref, bf16[512,1536]{1,0:T(8,128)(2,1)} %copy-done, ...), custom_call_target="tpu_custom_call", output_to_operand_aliasing={{0}: (8, {}), {1}: (9, {}), {2}: (10, {}), {3}: (11, {}), {... | custom-call | bytes 1024 | tf_op jit(solution)/shard_map/joined_1/pallas_call | solution.py:92
  80.5 5.7 %joined_2.1 = (bf16[1536,1536]{1,0:T(8,128)(2,1)}, bf16[1536,1536]{1,0:T(8,128)(2,1)}, f32[512,1536]{1,0:T(8,128)}, f32[512,1536]{1,0:T(8,128)}, bf16[512,1536]{1,0:T(8,128)(2,1)}) custom-call(s32[4]{0:T(128)} %pad_add_fusion.where_ref, bf16[512,1536]{1,0:T(8,128)(2,1)} %copy-done, ...), custom_call_target="tpu_custom_call", output_to_operand_aliasing={{0}: (8, {}), {1}: (9, {}), {2}: (10, {}), {3}: (11, {}), {... | custom-call | bytes 1024 | tf_op jit(solution)/shard_map/joined_2/pallas_call | solution.py:92
  86.8 1.5 collective-permute-done.12.refs_6_
  89.8 5.7 %joined_3.1 = (bf16[1536,1536]{1,0:T(8,128)(2,1)}, bf16[1536,1536]{1,0:T(8,128)(2,1)}, f32[512,1536]{1,0:T(8,128)}, f32[512,1536]{1,0:T(8,128)}, bf16[512,1536]{1,0:T(8,128)(2,1)}) custom-call(s32[4]{0:T(128)} %pad_add_fusion.where_ref, bf16[512,1536]{1,0:T(8,128)(2,1)} %copy-done, ...), custom_call_target="tpu_custom_call", output_to_operand_aliasing={{0}: (10, {}), {1}: (11, {}), {2}: (12, {}), {3}: (13, {}),... | custom-call | bytes 1024 | tf_op jit(solution)/shard_map/joined_3/pallas_call | solution.py:92
  96.3 3.4 %collective-permute-start.14 = (bf16[16,1536]{1,0:T(8,128)(2,1)S(1)}, bf16[16,1536]{1,0:T(8,128)(2,1)S(1)}, u32[]{:S(2)}, u32[]{:S(2)}) collective-permute-start(bf16[16,1536]{1,0:T(8,128)(2,1)S(1)} %get-tuple-element.185), channel_id=1, source_target_pairs={{0,8},{8,16},{16,24},{1,9},{9,17},{17,25},{2,10},{10,18},{18,26},{... | collective-permute-start | bytes 147464 | tf_op jit(solution)/shard_map/ppermute | solution.py:254
  101.5 4.2 %collective-permute-done.15.high_ref = bf16[16,1536]{1,0:T(8,128)(2,1)S(1)} collective-permute-done((bf16[16,1536]{1,0:T(8,128)(2,1)S(1)}, bf16[16,1536]{1,0:T(8,128)(2,1)S(1)}, u32[]{:S(2)}, u32[]{:S(2)}) %collective-permute-start.15) | collective-permute-done | bytes 49184 | tf_op jit(solution)/shard_map/ppermute | solution.py:255
  106.4 12.3 %conv_forward.1 = (bf16[512,1536]{1,0:T(8,128)(2,1)}, f32[512,1536]{1,0:T(8,128)}) custom-call(bf16[512,1536]{1,0:T(8,128)(2,1)} %get-tuple-element.121.glu_ref, bf16[16,1536]{1,0:T(8,128)(2,1)} %copy-done.14, bf16[16,1536]{1,0:T(8,128)(2,1)} %copy-done.15, f32[31,1536]{1,0:T(8,128)} %taps_ref.9), custom_call_target="tpu_custom_call" | custom-call | bytes 1024 | tf_op jit(solution)/shard_map/conv_forward/pallas_call | solution.py:159
  118.7 6.5 %fusion.18.grad_ref = bf16[512,1536]{1,0:T(8,128)(2,1)S(1)} fusion(f32[512,1536]{1,0:T(8,128)} %get-tuple-element.126, bf16[512,1536]{1,0:T(8,128)(2,1)} %get-tuple-element.125, bf16[1536,1536]{1,0:T(8,128)(2,1)} %all-gather.2.cloned.1.call-done), kind=kOutput, calls=%fused_computation.29 | convolution fusion | flops 2417491968 | bytes 11010048 | tf_op jit(solution)/shard_map/dot_general | solution.py:350
  125.3 3.5 %collective-permute-start.16 = (bf16[16,1536]{1,0:T(8,128)(2,1)S(1)}, bf16[16,1536]{1,0:T(8,128)(2,1)S(1)}, u32[]{:S(2)}, u32[]{:S(2)}) collective-permute-start(bf16[16,1536]{1,0:T(8,128)(2,1)S(1)} %get-tuple-element.183), channel_id=1, source_target_pairs={{0,8},{8,16},{16,24},{1,9},{9,17},{17,25},{2,10},{10,18},{18,26},{... | collective-permute-start | bytes 147464 | tf_op jit(solution)/shard_map/ppermute | solution.py:254
  128.7 1.5 collective-permute-start.17
  130.2 4.3 %convolution_convert_fusion = bf16[1536,1536]{1,0:T(8,128)(2,1)} fusion(bf16[512,1536]{1,0:T(8,128)(2,1)S(1)} %copy-done.35, bf16[512,1536]{1,0:T(8,128)(2,1)S(1)} %copy-done.13), kind=kOutput, calls=%fused_computation | convolution fusion | flops 2418278400 | bytes 7864320 | tf_op jit(solution)/shard_map/dot_general | solution.py:260
  135.3 8.0 %conv_backward_3.1 = (bf16[512,384]{1,0:T(8,128)(2,1)}, bf16[512,384]{1,0:T(8,128)(2,1)}, bf16[512,1536]{1,0:T(8,128)(2,1)}, bf16[512,1536]{1,0:T(8,128)(2,1)}, f32[32,1536]{1,0:T(8,128)}) custom-call(s32[4]{0:T(128)} %pad_add_fusion.where_ref, bf16[512,1536]{1,0:T(8,128)(2,1)} %copy-done.6, bf16[16,1536]{1,0:T(8,128)(2,1)} %copy-done.18, ...), custom_call_target="tpu_custom_call" | custom-call | bytes 1024 | tf_op jit(solution)/shard_map/conv_backward_3/pallas_call | solution.py:231
  143.4 8.2 %conv_backward_1.1 = (bf16[512,384]{1,0:T(8,128)(2,1)}, bf16[512,384]{1,0:T(8,128)(2,1)}, bf16[512,1536]{1,0:T(8,128)(2,1)}, bf16[512,1536]{1,0:T(8,128)(2,1)}, f32[32,1536]{1,0:T(8,128)}) custom-call(s32[4]{0:T(128)} %pad_add_fusion.where_ref, bf16[512,1536]{1,0:T(8,128)(2,1)} %copy-done.6, ...), custom_call_target="tpu_custom_call", output_to_operand_aliasing={{2}: (10, {}), {3}: (11, {}), {4}: (12, {})} | custom-call | bytes 1024 | tf_op jit(solution)/shard_map/conv_backward_1/pallas_call | solution.py:231
  153.2 2.1 fusion.21
  156.1 8.0 %conv_backward_2.1 = (bf16[512,384]{1,0:T(8,128)(2,1)}, bf16[512,384]{1,0:T(8,128)(2,1)}, bf16[512,1536]{1,0:T(8,128)(2,1)}, bf16[512,1536]{1,0:T(8,128)(2,1)}, f32[32,1536]{1,0:T(8,128)}) custom-call(s32[4]{0:T(128)} %pad_add_fusion.where_ref, bf16[512,1536]{1,0:T(8,128)(2,1)} %copy-done.6, ...), custom_call_target="tpu_custom_call", output_to_operand_aliasing={{2}: (10, {}), {3}: (11, {}), {4}: (12, {})} | custom-call | bytes 1024 | tf_op jit(solution)/shard_map/conv_backward_2/pallas_call | solution.py:231
  165.3 2.1 fusion.22
  167.3 3.1 %collective-permute-start.21 = (bf16[1536,384]{1,0:T(8,128)(2,1)}, bf16[1536,384]{1,0:T(8,128)(2,1)}, u32[]{:S(2)}, u32[]{:S(2)}) collective-permute-start(bf16[1536,384]{1,0:T(8,128)(2,1)} %fusion.22), channel_id=1, source_target_pairs={{0,8},{1,9},{2,10},{3,11},{4,12},{5,13},{6,14},{7,15},{8,0},{9,1},... | collective-permute-start | bytes 3538952 | tf_op jit(solution)/shard_map/ppermute | solution.py:39
  170.4 8.0 %conv_backward_0.1 = (bf16[512,384]{1,0:T(8,128)(2,1)}, bf16[512,384]{1,0:T(8,128)(2,1)}, bf16[512,1536]{1,0:T(8,128)(2,1)}, bf16[512,1536]{1,0:T(8,128)(2,1)}, f32[32,1536]{1,0:T(8,128)}) custom-call(s32[4]{0:T(128)} %pad_add_fusion.where_ref, bf16[512,1536]{1,0:T(8,128)(2,1)} %copy-done.6, ...), custom_call_target="tpu_custom_call", output_to_operand_aliasing={{2}: (10, {}), {3}: (11, {}), {4}: (12, {})} | custom-call | bytes 1024 | tf_op jit(solution)/shard_map/conv_backward_0/pallas_call | solution.py:231
  181.1 5.0 %fusion.33 = f32[512,1536]{1,0:T(8,128)S(1)} fusion(bf16[512,1536]{1,0:T(8,128)(2,1)S(1)} %copy-done.8, bf16[1536,1536]{1,0:T(8,128)(2,1)} %get-tuple-element.162), kind=kOutput, calls=%fused_computation.70 | convolution fusion | flops 2415919104 | bytes 9437184 | tf_op jit(solution)/shard_map/dot_general | solution.py:379
  186.1 4.5 %fusion.9 = (f32[1536]{0:T(1024)S(1)}, f32[512,1536]{1,0:T(8,128)}) fusion(bf16[1,512,1536]{2,1,0:T(8,128)(2,1)S(1)} %copy-done.4, f32[512]{0:T(512)S(1)} %add_rsqrt_fusion, f32[512]{0:T(512)S(1)} %broadcast_multiply_fusion.2, f32[512,1536]{1,0:T(8,128)S(1)} %fusion.33, bf16[512,1536]{1,0:T(8,128)(2,1)S(1)} %copy-done.7, bf16[1536,1536]{1,0:T(8,128)(2,1)S(1)} %bitcast.101), kind=kOutput, calls=%fused_computation.16 | convolution fusion | flops 2420636160 | bytes 14166016 | tf_op jit(solution)/shard_map/dot_general | solution.py:377
  191.7 19.3 %collective-permute-done.21 = bf16[1536,384]{1,0:T(8,128)(2,1)} collective-permute-done((bf16[1536,384]{1,0:T(8,128)(2,1)}, bf16[1536,384]{1,0:T(8,128)(2,1)}, u32[]{:S(2)}, u32[]{:S(2)}) %collective-permute-start.21) | collective-permute-done | bytes 1179680 | tf_op jit(solution)/shard_map/ppermute | solution.py:39
  211.1 4.1 %fusion.24 = bf16[1536,384]{1,0:T(8,128)(2,1)} fusion(f32[1536,384]{1,0:T(8,128)S(1)} %fusion.31, bf16[1536,512]{0,1:T(8,128)(2,1)S(1)} %bitcast.95, bf16[512,384]{1,0:T(8,128)(2,1)S(1)} %copy-done.23, bf16[1536,384]{1,0:T(8,128)(2,1)} %collective-permute-done.24, bf16[1536,384]{1,0:T(8,128)(2,1)S(1)} %collective-permute-done.23, ...), kind=kOutput, calls=%fused_computation.35 | convolution fusion | flops 608698368 | bytes 9043968 | tf_op jit(solution)/shard_map/dot_general | solution.py:368
  216.3 1.5 collective-permute-start.31
  219.9 3.0 %multiply_reduce_fusion = (f32[512]{0:T(512)S(1)}, f32[512]{0:T(512)S(1)}) fusion(f32[512,1536]{1,0:T(8,128)} %get-tuple-element.166, f32[1536]{0:T(1024)S(1)} %copy-done.34, f32[512]{0:T(512)S(1)} %add_rsqrt_fusion, f32[512]{0:T(512)S(1)} %broadcast_multiply_fusion.2, bf16[1,512,1536]{2,1,0:T(8,128)(2,1)S(1)} %copy-done.5), kind=kLoop, calls=%fused_computation.36 | loop fusion | flops 5504000 | bytes 4732928 | tf_op jit(solution)/shard_map/reduce_sum | solution.py:390
  223.1 7.0 %collective-permute-start.25 = (bf16[384,384]{1,0:T(8,128)(2,1)S(1)}, bf16[384,384]{1,0:T(8,128)(2,1)S(1)}, u32[]{:S(2)}, u32[]{:S(2)}) collective-permute-start(bf16[384,384]{1,0:T(8,128)(2,1)S(1)} %get-tuple-element.189), channel_id=1, source_target_pairs={{0,4},{1,5},{2,6},{3,7},{4,0},{5,1},{6,2},{7,3},{8,12},{9,13},{10,... | collective-permute-start | bytes 884744 | tf_op jit(solution)/shard_map/ppermute | solution.py:39
  231.5 5.7 %collective-permute-done.29 = f32[32,1536]{1,0:T(8,128)S(1)} collective-permute-done((f32[32,1536]{1,0:T(8,128)S(1)}, f32[32,1536]{1,0:T(8,128)S(1)}, u32[]{:S(2)}, u32[]{:S(2)}) %collective-permute-start.29) | collective-permute-done | bytes 196640 | tf_op jit(solution)/shard_map/ppermute | solution.py:39
  237.2 3.9 %collective-permute-start.27 = (bf16[384,384]{1,0:T(8,128)(2,1)S(1)}, bf16[384,384]{1,0:T(8,128)(2,1)S(1)}, u32[]{:S(2)}, u32[]{:S(2)}) collective-permute-start(bf16[384,384]{1,0:T(8,128)(2,1)S(1)} %get-tuple-element.187), channel_id=1, source_target_pairs={{0,6},{1,7},{2,0},{3,1},{4,2},{5,3},{6,4},{7,5},{8,14},{9,15},{10,... | collective-permute-start | bytes 884744 | tf_op jit(solution)/shard_map/ppermute | solution.py:39
  244.2 6.4 %collective-permute-done.25 = bf16[384,384]{1,0:T(8,128)(2,1)S(1)} collective-permute-done((bf16[384,384]{1,0:T(8,128)(2,1)S(1)}, bf16[384,384]{1,0:T(8,128)(2,1)S(1)}, u32[]{:S(2)}, u32[]{:S(2)}) %collective-permute-start.25) | collective-permute-done | bytes 294944 | tf_op jit(solution)/shard_map/ppermute | solution.py:39
  253.4 2.4 fusion.15
  256.7 2.5 collective-permute-done.35.refs_6_
  264.6 4.9 %collective-permute-done.41 = f32[32,1536]{1,0:T(8,128)S(1)} collective-permute-done((f32[32,1536]{1,0:T(8,128)S(1)}, f32[32,1536]{1,0:T(8,128)S(1)}, u32[]{:S(2)}, u32[]{:S(2)}) %collective-permute-start.41) | collective-permute-done | bytes 196640 | tf_op jit(solution)/shard_map/ppermute | solution.py:39
  269.6 6.6 %fusion.25 = bf16[1,512,1536]{2,1,0:T(8,128)(2,1)} fusion(bf16[512,1536]{1,0:T(8,128)(2,1)} %get-tuple-element.127, bf16[1536,1536]{1,0:T(8,128)(2,1)} %all-gather.2.cloned.1.call-done, bf16[1,512,1536]{2,1,0:T(8,128)(2,1)S(1)} %copy-done.5), kind=kOutput, calls=%fused_computation.37 | convolution fusion | flops 2418278400 | bytes 9437184 | tf_op jit(solution)/shard_map/dot_general | solution.py:356
  276.2 2.1 collective-permute-done.42
  280.5 3.4 %final.1 = (f32[192,3072]{1,0:T(8,128)}, f32[192,1536]{1,0:T(8,128)}) custom-call(s32[4]{0:T(128)} %pad_add_fusion.where_ref, bf16[2,192,384]{2,1,0:T(8,128)(2,1)} %copy-done.16, bf16[2,192,384]{2,1,0:T(8,128)(2,1)} %copy-done.27, bf16[2,192,384]{2,1,0:T(8,128)(2,1)} %copy-done.28, bf16[2,192,384]{2,1,0:T(8,128)(2,1)} %copy-done.29, ...), custom_call_target="tpu_custom_call" | custom-call | bytes 1024 | tf_op jit(solution)/shard_map/final/pallas_call | solution.py:280
  (177 shorter events, 40.6 us)
Async XLA Ops:
  7.2 111.5 %all-gather.2.cloned.1.call-start = ((), (), s32[]{:S(2)}) async-start(), calls=%async_computation.1 | async-start | bytes 5308416 | tf_op jit(solution)/shard_map/all_gather | solution.py:326
  9.1 24.8 %collective-permute-start.2 = (bf16[2,192,384]{2,1,0:T(8,128)(2,1)}, bf16[2,192,384]{2,1,0:T(8,128)(2,1)S(1)}, u32[]{:S(2)}, u32[]{:S(2)}) collective-permute-start(bf16[2,192,384]{2,1,0:T(8,128)(2,1)} %pad_maximum_fusion.1), channel_id=1, source_target_pairs={{0,4},{1,5},{2,6},{3,7},{4,0},{5,1},{6,2},{7,3},{8,12},{9,13},{10,... | collective-permute-start | bytes 884744 | tf_op jit(solution)/shard_map/ppermute | solution.py:39
  13.2 20.7 %collective-permute-start = (bf16[2,192,384]{2,1,0:T(8,128)(2,1)}, bf16[2,192,384]{2,1,0:T(8,128)(2,1)S(1)}, u32[]{:S(2)}, u32[]{:S(2)}) collective-permute-start(bf16[2,192,384]{2,1,0:T(8,128)(2,1)} %pad_maximum_fusion.1), channel_id=1, source_target_pairs={{0,2},{1,3},{2,4},{3,5},{4,6},{5,7},{6,0},{7,1},{8,10},{9,11},{10,... | collective-permute-start | bytes 884744 | tf_op jit(solution)/shard_map/ppermute | solution.py:39
  14.7 20.0 %collective-permute-start.1 = (bf16[2,192,384]{2,1,0:T(8,128)(2,1)}, bf16[2,192,384]{2,1,0:T(8,128)(2,1)}, u32[]{:S(2)}, u32[]{:S(2)}) collective-permute-start(bf16[2,192,384]{2,1,0:T(8,128)(2,1)} %pad_maximum_fusion.1), channel_id=1, source_target_pairs={{0,6},{1,7},{2,0},{3,1},{4,2},{5,3},{6,4},{7,5},{8,14},{9,15},{10,... | collective-permute-start | bytes 884744 | tf_op jit(solution)/shard_map/ppermute | solution.py:39
  17.0 19.7 %collective-permute-start.3 = (bf16[192,3072]{1,0:T(8,128)(2,1)}, bf16[192,3072]{1,0:T(8,128)(2,1)S(1)}, u32[]{:S(2)}, u32[]{:S(2)}) collective-permute-start(bf16[192,3072]{1,0:T(8,128)(2,1)} %refs_1_.7), channel_id=1, source_target_pairs={{0,1},{1,0},{2,3},{3,2},{4,5},{5,4},{6,7},{7,6},{8,9},{9,8},{10,11... | collective-permute-start | bytes 3538952 | tf_op jit(solution)/shard_map/ppermute | solution.py:39
  23.7 45.3 %copy-start = (bf16[512,1536]{1,0:T(8,128)(2,1)}, bf16[512,1536]{1,0:T(8,128)(2,1)S(1)}, u32[]{:S(2)}) copy-start(bf16[512,1536]{1,0:T(8,128)(2,1)S(1)} %get-tuple-element.93.lifted_ref) | copy-start | bytes 4718596
  37.7 177.5 %reduce-scatter.2.cloned.1.call-start = ((), (), s32[]{:S(2)}) async-start(), calls=%async_computation.2 | async-start | bytes 5308416 | tf_op jit(solution)/shard_map/reduce_scatter | solution.py:355
  37.7 23.7 %collective-permute-start.6 = (bf16[512,1536]{1,0:T(8,128)(2,1)S(1)}, bf16[512,1536]{1,0:T(8,128)(2,1)S(1)}, u32[]{:S(2)}, u32[]{:S(2)}) collective-permute-start(bf16[512,1536]{1,0:T(8,128)(2,1)S(1)} %get-tuple-element.93.lifted_ref), channel_id=1, source_target_pairs={{0,1},{1,0},{2,3},{3,2},{4,5},{5,4},{6,7},{7,6},{8,9},{9,8},{10,11... | collective-permute-start | bytes 4718600 | tf_op jit(solution)/shard_map/ppermute | solution.py:39
  37.7 22.4 %collective-permute-start.4 = (bf16[3,2,192,384]{3,2,1,0:T(8,128)(2,1)}, bf16[3,2,192,384]{3,2,1,0:T(8,128)(2,1)}, u32[]{:S(2)}, u32[]{:S(2)}) collective-permute-start(bf16[3,2,192,384]{3,2,1,0:T(8,128)(2,1)} %pad_maximum_fusion.refs_4_), channel_id=1, source_target_pairs={{0,8},{1,9},{2,10},{3,11},{4,12},{5,13},{6,14},{7,15},{8,0},{9,1},... | collective-permute-start | bytes 2654216 | tf_op jit(solution)/shard_map/ppermute | solution.py:39
  39.3 22.1 %collective-permute-start.5 = (bf16[3,2,192,384]{3,2,1,0:T(8,128)(2,1)}, bf16[3,2,192,384]{3,2,1,0:T(8,128)(2,1)}, u32[]{:S(2)}, u32[]{:S(2)}) collective-permute-start(bf16[3,2,192,384]{3,2,1,0:T(8,128)(2,1)} %pad_maximum_fusion.refs_4_), channel_id=1, source_target_pairs={{0,16},{1,17},{2,18},{3,19},{4,20},{5,21},{6,22},{7,23},{8,24},{9,... | collective-permute-start | bytes 2654216 | tf_op jit(solution)/shard_map/ppermute | solution.py:39
  40.8 20.6 %collective-permute-start.7 = (bf16[3,2,192,384]{3,2,1,0:T(8,128)(2,1)}, bf16[3,2,192,384]{3,2,1,0:T(8,128)(2,1)S(1)}, u32[]{:S(2)}, u32[]{:S(2)}) collective-permute-start(bf16[3,2,192,384]{3,2,1,0:T(8,128)(2,1)} %pad_maximum_fusion.refs_4_), channel_id=1, source_target_pairs={{0,1},{1,0},{2,3},{3,2},{4,5},{5,4},{6,7},{7,6},{8,9},{9,8},{10,11... | collective-permute-start | bytes 2654216 | tf_op jit(solution)/shard_map/ppermute | solution.py:39
  62.3 12.5 %collective-permute-start.11 = (bf16[3,2,192,384]{3,2,1,0:T(8,128)(2,1)}, bf16[3,2,192,384]{3,2,1,0:T(8,128)(2,1)}, u32[]{:S(2)}, u32[]{:S(2)}) collective-permute-start(bf16[3,2,192,384]{3,2,1,0:T(8,128)(2,1)} %collective-permute-done.4.refs_4_), channel_id=1, source_target_pairs={{0,1},{1,0},{2,3},{3,2},{4,5},{5,4},{6,7},{7,6},{8,9},{9,8},{10,11... | collective-permute-start | bytes 2654216 | tf_op jit(solution)/shard_map/ppermute | solution.py:39
  62.3 18.2 %collective-permute-start.10 = (bf16[3,2,192,384]{3,2,1,0:T(8,128)(2,1)}, bf16[3,2,192,384]{3,2,1,0:T(8,128)(2,1)}, u32[]{:S(2)}, u32[]{:S(2)}) collective-permute-start(bf16[3,2,192,384]{3,2,1,0:T(8,128)(2,1)} %collective-permute-done.5.refs_4_), channel_id=1, source_target_pairs={{0,1},{1,0},{2,3},{3,2},{4,5},{5,4},{6,7},{7,6},{8,9},{9,8},{10,11... | collective-permute-start | bytes 2654216 | tf_op jit(solution)/shard_map/ppermute | solution.py:39
  66.5 19.7 %collective-permute-start.8 = (bf16[3,2,96,384]{3,2,1,0:T(8,128)(2,1)}, bf16[3,2,96,384]{3,2,1,0:T(8,128)(2,1)}, u32[]{:S(2)}, u32[]{:S(2)}) collective-permute-start(bf16[3,2,96,384]{3,2,1,0:T(8,128)(2,1)} %slice.27), channel_id=1, source_target_pairs={{0,16},{1,17},{2,18},{3,19},{4,20},{5,21},{6,22},{7,23},{8,24},{9,... | collective-permute-start | bytes 1327112 | tf_op jit(solution)/shard_map/ppermute | solution.py:39
  68.0 18.2 %collective-permute-start.9 = (bf16[3,2,96,384]{3,2,1,0:T(8,128)(2,1)}, bf16[3,2,96,384]{3,2,1,0:T(8,128)(2,1)}, u32[]{:S(2)}, u32[]{:S(2)}) collective-permute-start(bf16[3,2,96,384]{3,2,1,0:T(8,128)(2,1)} %slice.28), channel_id=1, source_target_pairs={{0,8},{1,9},{2,10},{3,11},{4,12},{5,13},{6,14},{7,15},{8,0},{9,1},... | collective-permute-start | bytes 1327112 | tf_op jit(solution)/shard_map/ppermute | solution.py:39
  86.2 2.1 collective-permute-start.12
  86.3 2.6 collective-permute-start.13
  96.3 5.2 %collective-permute-start.14 = (bf16[16,1536]{1,0:T(8,128)(2,1)S(1)}, bf16[16,1536]{1,0:T(8,128)(2,1)S(1)}, u32[]{:S(2)}, u32[]{:S(2)}) collective-permute-start(bf16[16,1536]{1,0:T(8,128)(2,1)S(1)} %get-tuple-element.185), channel_id=1, source_target_pairs={{0,8},{8,16},{16,24},{1,9},{9,17},{17,25},{2,10},{10,18},{18,26},{... | collective-permute-start | bytes 147464 | tf_op jit(solution)/shard_map/ppermute | solution.py:254
  99.8 6.0 %collective-permute-start.15 = (bf16[16,1536]{1,0:T(8,128)(2,1)S(1)}, bf16[16,1536]{1,0:T(8,128)(2,1)S(1)}, u32[]{:S(2)}, u32[]{:S(2)}) collective-permute-start(bf16[16,1536]{1,0:T(8,128)(2,1)S(1)} %get-tuple-element.184), channel_id=1, source_target_pairs={{8,0},{16,8},{24,16},{9,1},{17,9},{25,17},{10,2},{18,10},{26,18},{... | collective-permute-start | bytes 147464 | tf_op jit(solution)/shard_map/ppermute | solution.py:255
  125.3 9.3 %collective-permute-start.16 = (bf16[16,1536]{1,0:T(8,128)(2,1)S(1)}, bf16[16,1536]{1,0:T(8,128)(2,1)S(1)}, u32[]{:S(2)}, u32[]{:S(2)}) collective-permute-start(bf16[16,1536]{1,0:T(8,128)(2,1)S(1)} %get-tuple-element.183), channel_id=1, source_target_pairs={{0,8},{8,16},{16,24},{1,9},{9,17},{17,25},{2,10},{10,18},{18,26},{... | collective-permute-start | bytes 147464 | tf_op jit(solution)/shard_map/ppermute | solution.py:254
  128.7 6.0 %collective-permute-start.17 = (bf16[16,1536]{1,0:T(8,128)(2,1)S(1)}, bf16[16,1536]{1,0:T(8,128)(2,1)S(1)}, u32[]{:S(2)}, u32[]{:S(2)}) collective-permute-start(bf16[16,1536]{1,0:T(8,128)(2,1)S(1)} %get-tuple-element.182), channel_id=1, source_target_pairs={{8,0},{16,8},{24,16},{9,1},{17,9},{25,17},{10,2},{18,10},{26,18},{... | collective-permute-start | bytes 147464 | tf_op jit(solution)/shard_map/ppermute | solution.py:255
  143.3 8.9 %collective-permute-start.18 = (bf16[512,384]{1,0:T(8,128)(2,1)}, bf16[512,384]{1,0:T(8,128)(2,1)S(1)}, u32[]{:S(2)}, u32[]{:S(2)}) collective-permute-start(bf16[512,384]{1,0:T(8,128)(2,1)} %get-tuple-element.140), channel_id=1, source_target_pairs={{0,1},{1,0},{2,3},{3,2},{4,5},{5,4},{6,7},{7,6},{8,9},{9,8},{10,11... | collective-permute-start | bytes 1179656 | tf_op jit(solution)/shard_map/ppermute | solution.py:39
  151.5 12.8 %collective-permute-start.19 = (bf16[512,384]{1,0:T(8,128)(2,1)}, bf16[512,384]{1,0:T(8,128)(2,1)S(1)}, u32[]{:S(2)}, u32[]{:S(2)}) collective-permute-start(bf16[512,384]{1,0:T(8,128)(2,1)} %get-tuple-element.148), channel_id=1, source_target_pairs={{0,1},{1,0},{2,3},{3,2},{4,5},{5,4},{6,7},{7,6},{8,9},{9,8},{10,11... | collective-permute-start | bytes 1179656 | tf_op jit(solution)/shard_map/ppermute | solution.py:39
  155.3 55.8 %collective-permute-start.24 = (bf16[1536,384]{1,0:T(8,128)(2,1)}, bf16[1536,384]{1,0:T(8,128)(2,1)}, u32[]{:S(2)}, u32[]{:S(2)}) collective-permute-start(bf16[1536,384]{1,0:T(8,128)(2,1)} %fusion.21), channel_id=1, source_target_pairs={{0,24},{1,25},{2,26},{3,27},{4,28},{5,29},{6,30},{7,31},{8,16},{9,... | collective-permute-start | bytes 3538952 | tf_op jit(solution)/shard_map/ppermute | solution.py:39
  164.1 14.6 %collective-permute-start.22 = (bf16[512,384]{1,0:T(8,128)(2,1)}, bf16[512,384]{1,0:T(8,128)(2,1)S(1)}, u32[]{:S(2)}, u32[]{:S(2)}) collective-permute-start(bf16[512,384]{1,0:T(8,128)(2,1)} %get-tuple-element.155), channel_id=1, source_target_pairs={{0,1},{1,0},{2,3},{3,2},{4,5},{5,4},{6,7},{7,6},{8,9},{9,8},{10,11... | collective-permute-start | bytes 1179656 | tf_op jit(solution)/shard_map/ppermute | solution.py:39
  167.3 43.7 %collective-permute-start.21 = (bf16[1536,384]{1,0:T(8,128)(2,1)}, bf16[1536,384]{1,0:T(8,128)(2,1)}, u32[]{:S(2)}, u32[]{:S(2)}) collective-permute-start(bf16[1536,384]{1,0:T(8,128)(2,1)} %fusion.22), channel_id=1, source_target_pairs={{0,8},{1,9},{2,10},{3,11},{4,12},{5,13},{6,14},{7,15},{8,0},{9,1},... | collective-permute-start | bytes 3538952 | tf_op jit(solution)/shard_map/ppermute | solution.py:39
  178.4 12.3 %collective-permute-start.20 = (bf16[512,384]{1,0:T(8,128)(2,1)}, bf16[512,384]{1,0:T(8,128)(2,1)S(1)}, u32[]{:S(2)}, u32[]{:S(2)}) collective-permute-start(bf16[512,384]{1,0:T(8,128)(2,1)} %get-tuple-element.153), channel_id=1, source_target_pairs={{0,1},{1,0},{2,3},{3,2},{4,5},{5,4},{6,7},{7,6},{8,9},{9,8},{10,11... | collective-permute-start | bytes 1179656 | tf_op jit(solution)/shard_map/ppermute | solution.py:39
  180.7 30.3 %collective-permute-start.23 = (bf16[1536,384]{1,0:T(8,128)(2,1)S(1)}, bf16[1536,384]{1,0:T(8,128)(2,1)S(1)}, u32[]{:S(2)}, u32[]{:S(2)}) collective-permute-start(bf16[1536,384]{1,0:T(8,128)(2,1)S(1)} %fusion.23), channel_id=1, source_target_pairs={{0,16},{1,17},{2,18},{3,19},{4,20},{5,21},{6,22},{7,23},{8,24},{9,... | collective-permute-start | bytes 3538952 | tf_op jit(solution)/shard_map/ppermute | solution.py:39
  216.3 20.9 %collective-permute-start.31 = (bf16[48,1536]{1,0:T(8,128)(2,1)S(1)}, bf16[48,1536]{1,0:T(8,128)(2,1)S(1)}, u32[]{:S(2)}, u32[]{:S(2)}) collective-permute-start(bf16[48,1536]{1,0:T(8,128)(2,1)S(1)} %get-tuple-element.192), channel_id=1, source_target_pairs={{0,24},{1,25},{2,26},{3,27},{4,28},{5,29},{6,30},{7,31},{8,16},{9,... | collective-permute-start | bytes 442376 | tf_op jit(solution)/shard_map/ppermute | solution.py:39
  217.8 23.3 %collective-permute-start.32 = (bf16[48,1536]{1,0:T(8,128)(2,1)S(1)}, bf16[48,1536]{1,0:T(8,128)(2,1)S(1)}, u32[]{:S(2)}, u32[]{:S(2)}) collective-permute-start(bf16[48,1536]{1,0:T(8,128)(2,1)S(1)} %get-tuple-element.194), channel_id=1, source_target_pairs={{0,8},{1,9},{2,10},{3,11},{4,12},{5,13},{6,14},{7,15},{8,0},{9,1},... | collective-permute-start | bytes 442376 | tf_op jit(solution)/shard_map/ppermute | solution.py:39
  219.1 23.3 %collective-permute-start.33 = (bf16[48,1536]{1,0:T(8,128)(2,1)S(1)}, bf16[48,1536]{1,0:T(8,128)(2,1)S(1)}, u32[]{:S(2)}, u32[]{:S(2)}) collective-permute-start(bf16[48,1536]{1,0:T(8,128)(2,1)S(1)} %get-tuple-element.193), channel_id=1, source_target_pairs={{0,16},{1,17},{2,18},{3,19},{4,20},{5,21},{6,22},{7,23},{8,24},{9,... | collective-permute-start | bytes 442376 | tf_op jit(solution)/shard_map/ppermute | solution.py:39
  219.8 33.5 %copy-start.10 = (bf16[1,512,1536]{2,1,0:T(8,128)(2,1)S(1)}, bf16[1,512,1536]{2,1,0:T(8,128)(2,1)}, u32[]{:S(2)}) copy-start(bf16[1,512,1536]{2,1,0:T(8,128)(2,1)} %param.13) | copy-start | bytes 4718596
  222.9 30.5 %copy-start.9 = (f32[512,1536]{1,0:T(8,128)S(1)}, f32[512,1536]{1,0:T(8,128)}, u32[]{:S(2)}) copy-start(f32[512,1536]{1,0:T(8,128)} %get-tuple-element.166) | copy-start | bytes 9437188
  222.9 7.2 %collective-permute-start.28 = (f32[32,1536]{1,0:T(8,128)S(1)}, f32[32,1536]{1,0:T(8,128)S(1)}, u32[]{:S(2)}, u32[]{:S(2)}) collective-permute-start(f32[32,1536]{1,0:T(8,128)S(1)} %pad_maximum_fusion.3), channel_id=1, source_target_pairs={{0,1},{1,0},{2,3},{3,2},{4,5},{5,4},{6,7},{7,6},{8,9},{9,8},{10,11... | collective-permute-start | bytes 589832 | tf_op jit(solution)/shard_map/ppermute | solution.py:39
  223.1 27.5 %collective-permute-start.25 = (bf16[384,384]{1,0:T(8,128)(2,1)S(1)}, bf16[384,384]{1,0:T(8,128)(2,1)S(1)}, u32[]{:S(2)}, u32[]{:S(2)}) collective-permute-start(bf16[384,384]{1,0:T(8,128)(2,1)S(1)} %get-tuple-element.189), channel_id=1, source_target_pairs={{0,4},{1,5},{2,6},{3,7},{4,0},{5,1},{6,2},{7,3},{8,12},{9,13},{10,... | collective-permute-start | bytes 884744 | tf_op jit(solution)/shard_map/ppermute | solution.py:39
  230.1 7.1 %collective-permute-start.29 = (f32[32,1536]{1,0:T(8,128)S(1)}, f32[32,1536]{1,0:T(8,128)S(1)}, u32[]{:S(2)}, u32[]{:S(2)}) collective-permute-start(f32[32,1536]{1,0:T(8,128)S(1)} %add.165), channel_id=1, source_target_pairs={{0,8},{1,9},{2,10},{3,11},{4,12},{5,13},{6,14},{7,15},{8,0},{9,1},... | collective-permute-start | bytes 589832 | tf_op jit(solution)/shard_map/ppermute | solution.py:39
  237.2 18.6 %collective-permute-start.26 = (bf16[384,384]{1,0:T(8,128)(2,1)S(1)}, bf16[384,384]{1,0:T(8,128)(2,1)S(1)}, u32[]{:S(2)}, u32[]{:S(2)}) collective-permute-start(bf16[384,384]{1,0:T(8,128)(2,1)S(1)} %get-tuple-element.188), channel_id=1, source_target_pairs={{0,2},{1,3},{2,4},{3,5},{4,6},{5,7},{6,0},{7,1},{8,10},{9,11},{10,... | collective-permute-start | bytes 884744 | tf_op jit(solution)/shard_map/ppermute | solution.py:39
  237.2 19.5 %collective-permute-start.27 = (bf16[384,384]{1,0:T(8,128)(2,1)S(1)}, bf16[384,384]{1,0:T(8,128)(2,1)S(1)}, u32[]{:S(2)}, u32[]{:S(2)}) collective-permute-start(bf16[384,384]{1,0:T(8,128)(2,1)S(1)} %get-tuple-element.187), channel_id=1, source_target_pairs={{0,6},{1,7},{2,0},{3,1},{4,2},{5,3},{6,4},{7,5},{8,14},{9,15},{10,... | collective-permute-start | bytes 884744 | tf_op jit(solution)/shard_map/ppermute | solution.py:39
  241.1 10.8 %collective-permute-start.30 = (f32[32,1536]{1,0:T(8,128)S(1)}, f32[32,1536]{1,0:T(8,128)S(1)}, u32[]{:S(2)}, u32[]{:S(2)}) collective-permute-start(f32[32,1536]{1,0:T(8,128)S(1)} %add.166), channel_id=1, source_target_pairs={{0,16},{1,17},{2,18},{3,19},{4,20},{5,21},{6,22},{7,23},{8,24},{9,... | collective-permute-start | bytes 589832 | tf_op jit(solution)/shard_map/ppermute | solution.py:39
  243.4 13.3 %collective-permute-start.34 = (bf16[48,1536]{1,0:T(8,128)(2,1)S(1)}, bf16[48,1536]{1,0:T(8,128)(2,1)S(1)}, u32[]{:S(2)}, u32[]{:S(2)}) collective-permute-start(bf16[48,1536]{1,0:T(8,128)(2,1)S(1)} %add_convert_fusion.1.refs_4_), channel_id=1, source_target_pairs={{0,8},{1,9},{2,10},{3,11},{4,12},{5,13},{6,14},{7,15},{8,0},{9,1},... | collective-permute-start | bytes 442376 | tf_op jit(solution)/shard_map/ppermute | solution.py:39
  250.6 8.6 %collective-permute-start.35 = (bf16[48,1536]{1,0:T(8,128)(2,1)S(1)}, bf16[48,1536]{1,0:T(8,128)(2,1)S(1)}, u32[]{:S(2)}, u32[]{:S(2)}) collective-permute-start(bf16[48,1536]{1,0:T(8,128)(2,1)S(1)} %add_convert_fusion.1.refs_4_), channel_id=1, source_target_pairs={{0,16},{1,17},{2,18},{3,19},{4,20},{5,21},{6,22},{7,23},{8,24},{9,... | collective-permute-start | bytes 442376 | tf_op jit(solution)/shard_map/ppermute | solution.py:39
  251.9 7.3 %collective-permute-start.36 = (bf16[48,1536]{1,0:T(8,128)(2,1)S(1)}, bf16[48,1536]{1,0:T(8,128)(2,1)S(1)}, u32[]{:S(2)}, u32[]{:S(2)}) collective-permute-start(bf16[48,1536]{1,0:T(8,128)(2,1)S(1)} %add_convert_fusion.1.refs_4_), channel_id=1, source_target_pairs={{0,24},{1,25},{2,26},{3,27},{4,28},{5,29},{6,30},{7,31},{8,16},{9,... | collective-permute-start | bytes 442376 | tf_op jit(solution)/shard_map/ppermute | solution.py:39
  259.4 1.4 collective-permute-start.37
  259.5 10.0 %collective-permute-start.41 = (f32[32,1536]{1,0:T(8,128)S(1)}, f32[32,1536]{1,0:T(8,128)S(1)}, u32[]{:S(2)}, u32[]{:S(2)}) collective-permute-start(f32[32,1536]{1,0:T(8,128)S(1)} %add.167), channel_id=1, source_target_pairs={{0,4},{1,5},{2,6},{3,7},{4,0},{5,1},{6,2},{7,3},{8,12},{9,13},{10,... | collective-permute-start | bytes 589832 | tf_op jit(solution)/shard_map/ppermute | solution.py:39
  261.0 17.9 %collective-permute-start.38 = (bf16[2,192,384]{2,1,0:T(8,128)(2,1)S(1)}, bf16[2,192,384]{2,1,0:T(8,128)(2,1)S(1)}, u32[]{:S(2)}, u32[]{:S(2)}) collective-permute-start(bf16[2,192,384]{2,1,0:T(8,128)(2,1)S(1)} %pad_maximum_fusion.2.refs_0_), channel_id=1, source_target_pairs={{0,8},{1,9},{2,10},{3,11},{4,12},{5,13},{6,14},{7,15},{8,0},{9,1},... | collective-permute-start | bytes 884744 | tf_op jit(solution)/shard_map/ppermute | solution.py:39
  262.4 16.6 %collective-permute-start.39 = (bf16[2,192,384]{2,1,0:T(8,128)(2,1)S(1)}, bf16[2,192,384]{2,1,0:T(8,128)(2,1)S(1)}, u32[]{:S(2)}, u32[]{:S(2)}) collective-permute-start(bf16[2,192,384]{2,1,0:T(8,128)(2,1)S(1)} %pad_maximum_fusion.2.refs_0_), channel_id=1, source_target_pairs={{0,16},{1,17},{2,18},{3,19},{4,20},{5,21},{6,22},{7,23},{8,24},{9,... | collective-permute-start | bytes 884744 | tf_op jit(solution)/shard_map/ppermute | solution.py:39
  263.1 15.9 %collective-permute-start.40 = (bf16[2,192,384]{2,1,0:T(8,128)(2,1)S(1)}, bf16[2,192,384]{2,1,0:T(8,128)(2,1)S(1)}, u32[]{:S(2)}, u32[]{:S(2)}) collective-permute-start(bf16[2,192,384]{2,1,0:T(8,128)(2,1)S(1)} %pad_maximum_fusion.2.refs_0_), channel_id=1, source_target_pairs={{0,24},{1,25},{2,26},{3,27},{4,28},{5,29},{6,30},{7,31},{8,16},{9,... | collective-permute-start | bytes 884744 | tf_op jit(solution)/shard_map/ppermute | solution.py:39
  269.5 8.7 %collective-permute-start.42 = (f32[32,1536]{1,0:T(8,128)S(1)}, f32[32,1536]{1,0:T(8,128)S(1)}, u32[]{:S(2)}, u32[]{:S(2)}) collective-permute-start(f32[32,1536]{1,0:T(8,128)S(1)} %add.181), channel_id=1, source_target_pairs={{0,2},{1,3},{2,4},{3,5},{4,6},{5,7},{6,0},{7,1},{8,10},{9,11},{10,... | collective-permute-start | bytes 589832 | tf_op jit(solution)/shard_map/ppermute | solution.py:39
  (35 other events, 222.4 us)
Sparse Core Ops, SparseCore 0:
  36.9 56.6 all-gather.1
  134.9 59.7 reduce-scatter.1
